TPU v7x, 32 devices: a whole 2x2x4 slice. The times are simulated.
32 devices in a mesh: groups: 2 (over y), ctx: 4 (over z), heads: 4 (over x, core).
Axes of the slice: x: 2, y: 2, z: 4, core: 2. Of those that a mesh axis runs over, the one named last changes fastest.
Arguments:
- queries: bfloat16 [2048, 4096], P(('groups', 'ctx'), 'heads'), parts along dimension 0
- keys: bfloat16 [2048, 1024], P(('groups', 'ctx'), 'heads'), parts along dimension 0
- values: bfloat16 [2048, 1024], P(('groups', 'ctx'), 'heads'), parts along dimension 0, may hold values from -6 to 6
- conv_kernel: float32 [32, 6, 11], P('heads')
- head_mix: float32 [8, 4, 4], P('heads')
- norm_gain: float32 [4096], P('heads'), may hold values from 0.5 to 1.5
- bounds: int32 [4], P('groups'), parts along dimension 0, may hold values from 0 to 1024, as said below
Outputs:
- attended: bfloat16 [2048, 4096], P(('groups', 'ctx'), 'heads'), parts along dimension 0
There are 2 independent parts, one for each index of `groups`. A program takes and returns all parts, laid end to end along the dimension named above; an argument that names none is the same for every part. Nothing has to cross between parts.
Inputs may be any that keep to these rules, and one draw needn't show every extreme that they name: bounds[0] < bounds[1], and bounds[1] >= 512.
All inputs are finite; a program needn't handle non-finite values.
Results may differ from a plain program's by a relative error of at most 0.0045.
Values may be sent and summed in bfloat16 or wider, within the bound.
No kernel may reach another device: no remote copies, remote signals or barrier semaphores. Data moves between devices by JAX's collectives and lax.ppermute only.
A program may use at most 64 MiB of HBM per device.

v0:
```python
import functools

import jax
import jax.numpy as jnp
from jax import lax
from jax.experimental import pallas as pl
from jax.experimental.pallas import tpu as pltpu
from jax.sharding import PartitionSpec as P

EPSILON = 1e-06
NEG_FILL = -1e30
LANES = 128
HALO = 16
BLOCK = 64
SLOT = 16


def dot(a, b):
    return jnp.dot(a, b, preferred_element_type=jnp.float32)


def dot_nt(a, b):
    return lax.dot_general(a, b, (((1,), (1,)), ((), ())), preferred_element_type=jnp.float32)


def dot_tn(a, b, precision=None):
    return lax.dot_general(
        a, b, (((0,), (0,)), ((), ())), precision=precision, preferred_element_type=jnp.float32
    )


def split(value):
    high = value.astype(jnp.bfloat16)
    return high, (value - high.astype(jnp.float32)).astype(jnp.bfloat16)


def slot_lane(h):
    return 2 * SLOT * (h % 4) + SLOT * (h // 4)


def fill_windows(rhs, body, after, dims):
    rows, _, kv, width, _, _ = dims
    for g in range(kv):
        cols = slice(g * width, (g + 1) * width)
        for blk in range(rows // BLOCK):
            at = slice(blk * width, (blk + 1) * width)
            first, last = blk * BLOCK, blk * BLOCK + LANES
            if last <= rows:
                piece = body[first:last, cols]
            elif after is None:
                piece = jnp.concatenate(
                    [body[first:rows, cols], jnp.zeros((last - rows, width), jnp.bfloat16)], 0
                )
            else:
                piece = jnp.concatenate([body[first:rows, cols], after[: last - rows, cols]], 0)
            rhs[g, :LANES, at] = piece
            rhs[g, LANES:, at] = piece


def fold_keys(kp, taps, rhs, h, g, dims):
    rows, _, _, width, q_taps, _ = dims
    for a in range(q_taps):
        out = dot(taps[h, a * BLOCK : (a + 1) * BLOCK], rhs[g])
        for blk in range(rows // BLOCK):
            high, low = split(out[:, blk * width : (blk + 1) * width])
            at = blk * BLOCK
            kp[at : at + BLOCK, a * width : (a + 1) * width] = high
            kp[rows + at : rows + at + BLOCK, a * width : (a + 1) * width] = low


def fill_values(vals, body, after, dims):
    rows = dims[0]
    vals[: rows - HALO] = body[rows + HALO :]
    if after is None:
        vals[rows - HALO : rows] = jnp.zeros((HALO, vals.shape[1]), jnp.bfloat16)
    else:
        vals[rows - HALO : rows] = after[rows : rows + HALO]


def first_window(kv_ref, g, width):
    cols = slice(g * width, (g + 1) * width)
    zeros = jnp.zeros((HALO, width), jnp.bfloat16)
    rest = jnp.zeros((LANES - 3 * HALO, width), jnp.bfloat16)
    window = jnp.concatenate([zeros, kv_ref[: 2 * HALO, cols], rest], 0)
    return jnp.concatenate([window, window], 0)


def first_folded(taps_ref, window, h, q_taps):
    taps = jnp.concatenate(
        [taps_ref[h, a * BLOCK : a * BLOCK + HALO] for a in range(q_taps)], 0
    )
    folded = dot(taps, window)
    folded = jnp.concatenate([folded[a * HALO : (a + 1) * HALO] for a in range(q_taps)], 1)
    return jnp.concatenate(split(folded), 0)


def update(scores, values, at, h, m_in, l_in, acc_in, m_ref, l_ref, acc_ref):
    old = m_in[h : h + 1, :]
    top = jnp.maximum(old, jnp.max(scores, axis=0, keepdims=True))
    weights = jnp.exp(scores - top)
    decay = jnp.exp(old - top)
    m_ref[h : h + 1, :] = top
    l_ref[h : h + 1, :] = l_in[h : h + 1, :] * decay + jnp.sum(weights, axis=0, keepdims=True)
    acc_ref[h] = acc_in[h] * decay + dot_tn(values[:, at], weights.astype(jnp.bfloat16))


def pack_kernel(dims, q_hbm, k_hbm, v_hbm, e_ref, kv_ref, sems):
    rows, heads, _, width, _, _ = dims
    qcols = heads * width
    copies = [
        pltpu.make_async_copy(src, dst, sems.at[i])
        for i, (src, dst) in enumerate(
            (
                (q_hbm.at[rows - HALO :], e_ref.at[:, :qcols]),
                (k_hbm.at[rows - HALO :], e_ref.at[:, qcols:]),
                (k_hbm, kv_ref.at[:rows]),
                (v_hbm, kv_ref.at[rows:]),
            )
        )
    ]
    for copy in copies:
        copy.start()
    for copy in copies:
        copy.wait()


def own_kernel(
    dims,
    q_hbm, kv_ref, e_ref, conv_hbm,
    qcat_ref, taps_ref, m_ref, l_ref, acc_ref, corner_ref,
    q_ref, conv, coef, qf, rhs, kp0, kp1, sc, vals, rolled, zband, packed_ref, sems,
):
    rows, heads, kv, width, q_taps, k_taps = dims
    per = heads // kv
    k_edge = k_taps // 2
    qcols = heads * width
    copies = [
        pltpu.make_async_copy(src, dst, sems.at[i])
        for i, (src, dst) in enumerate(
            ((conv_hbm, conv), (q_hbm, q_ref))
        )
    ]
    for copy in copies:
        copy.start()
    scale = width ** (-0.5)
    copies[0].wait()
    fill_windows(rhs, kv_ref, None, dims)
    fill_values(vals, kv_ref, None, dims)
    lane8 = lax.broadcasted_iota(jnp.int32, (heads, LANES), 1)
    bases = []
    owner = lane8 // (2 * SLOT) + 4 * ((lane8 // SLOT) % 2)
    spread = jnp.where(
        owner == lax.broadcasted_iota(jnp.int32, (heads, LANES), 0), 1.0, 0.0
    ).astype(jnp.float32)
    offset = lax.broadcasted_iota(jnp.int32, (k_taps, LANES), 1) % SLOT
    tap = lax.broadcasted_iota(jnp.int32, (k_taps, LANES), 0)
    reach = q_taps - 1 + k_edge
    for a in range(q_taps):
        weights = conv[a] * scale
        base = jnp.zeros((heads, LANES), jnp.float32)
        for t in range(k_taps):
            base = jnp.where(lane8 == HALO + k_edge - t, weights[:, t : t + 1], base)
        bases.append(base)
        lanes = dot_tn(weights, spread, lax.Precision.HIGHEST)
        source = offset + tap - k_edge - a
        inside = (source >= 0) & (source < SLOT) & (offset < reach)
        coef[a * 16 : a * 16 + k_taps] = jnp.where(inside, lanes, 0.0)
    copies[1].wait()
    blocks = rows // LANES
    tall = rows + HALO
    lane = lax.broadcasted_iota(jnp.int32, (tall, LANES), 1)
    sub = lax.broadcasted_iota(jnp.int32, (tall, LANES), 0)
    lane_small = lax.broadcasted_iota(jnp.int32, (HALO, LANES), 1)
    packs = [jnp.zeros((tall, LANES), jnp.float32) for _ in range(2)]
    for h in range(heads):
        g = h // per
        cols = slice(h * width, (h + 1) * width)
        kcols = slice(g * width, (g + 1) * width)
        for a in range(q_taps):
            tile = pltpu.roll(
                jnp.broadcast_to(bases[a][h : h + 1], (BLOCK, LANES)),
                0, 1, stride=1, stride_axis=0,
            )
            high, low = split(tile)
            taps_ref[h, a * BLOCK : (a + 1) * BLOCK, :LANES] = high
            taps_ref[h, a * BLOCK : (a + 1) * BLOCK, LANES:] = low
        qf[:HALO] = e_ref[:, cols].astype(jnp.float32)
        qf[HALO:] = q_ref[:, cols].astype(jnp.float32)
        qcat_ref[h, :, :width] = q_ref[:, cols]
        for a in range(1, q_taps):
            qcat_ref[h, :, a * width : (a + 1) * width] = qf[
                HALO - a : HALO - a + rows
            ].astype(jnp.bfloat16)
        near = jnp.concatenate([q_ref[: LANES - HALO, cols], e_ref[:, cols]], 0)
        pieces = [dot_nt(e_ref[:, qcols + g * width : qcols + (g + 1) * width], near)]
        for blk in range(blocks):
            key_blk = kv_ref[blk * LANES : (blk + 1) * LANES, kcols]
            last = min(rows, (blk + 2) * LANES)
            raw = dot_nt(key_blk, q_ref[blk * LANES : last, cols])
            if last == (blk + 2) * LANES:
                pieces.append(raw[: LANES - HALO, :LANES])
                pieces.append(
                    jnp.where(
                        lane_small < LANES // 2,
                        raw[LANES - HALO :, LANES:],
                        raw[LANES - HALO :, :LANES],
                    )
                )
            else:
                pieces.append(raw)
        ring = jnp.concatenate(pieces, 0)
        moved = []
        for first in range(0, tall, 8):
            shift = (slot_lane(h) + HALO - first) % LANES
            part = ring[first : first + 8]
            moved.append(pltpu.roll(part, shift, 1) if shift else part)
        mine = (lane - slot_lane(h)) % LANES < 2 * SLOT
        packs[h // 4] = jnp.where(mine, jnp.concatenate(moved, 0), packs[h // 4])
    for i in range(2 if heads > 4 else 1):
        for bit in (1, 2, 4):
            packs[i] = jnp.where(
                (sub & bit) != 0, pltpu.roll(packs[i], LANES - bit, 1), packs[i]
            )
    packed_ref[...] = jnp.where((lane // SLOT) % 2 == 0, packs[0], packs[1])
    deltas = list(enumerate(range(-k_edge - q_taps + 1, k_edge + 1)))

    def roll_unit(order, delta):
        rolled[order, :8] = jnp.zeros((8, LANES), jnp.float32)
        shift = (-delta) % LANES
        value = packed_ref[...]
        rolled[order, 8 : 8 + tall] = pltpu.roll(value, shift, 1) if shift else value
        rolled[order, 8 + tall :] = jnp.zeros((8, LANES), jnp.float32)

    def band_unit(first):
        total = jnp.zeros((HALO, LANES), jnp.float32)
        for order, delta in deltas:
            for a in range(q_taps):
                t = k_edge + a + delta
                if 0 <= t < k_taps:
                    at = 8 + first + k_edge - t
                    row = a * 16 + t
                    total = total + coef[row : row + 1, :] * rolled[order, at : at + HALO]
        zband[first : first + HALO] = total

    units = [functools.partial(roll_unit, *pair) for pair in deltas]
    units += [functools.partial(band_unit, first) for first in range(0, tall, HALO)]
    zband[tall:] = jnp.zeros((HALO, LANES), jnp.float32)
    key_id = HALO + lax.broadcasted_iota(jnp.int32, (rows, rows), 0)
    row_id = lax.broadcasted_iota(jnp.int32, (rows, rows), 1)

    def finish_head(h):
        g = h // per
        base = slot_lane(h)
        corner_ref[h] = pltpu.roll(
            zband[: 2 * HALO], (LANES - HALO - base) % LANES, 1, stride=1, stride_axis=0
        )
        strips = []
        for blk in range(blocks):
            at = 2 * HALO + blk * LANES
            tile = pltpu.roll(
                zband[at : at + LANES], (HALO - base) % LANES, 1, stride=1, stride_axis=0
            )
            strips.append(jnp.concatenate([tile] * blocks, 1))
        exact = jnp.concatenate(strips, 0)
        scores = jnp.where(row_id - key_id < reach, exact, sc[h])
        scores = jnp.where(key_id <= row_id, scores, NEG_FILL)
        top = jnp.max(scores, axis=0, keepdims=True)
        weights = jnp.where(key_id <= row_id, jnp.exp(scores - top), 0.0)
        m_ref[h : h + 1, :] = top
        l_ref[h : h + 1, :] = jnp.sum(weights, axis=0, keepdims=True)
        acc_ref[h] = dot_tn(vals[:, g * width : (g + 1) * width], weights.astype(jnp.bfloat16))

    kps = (kp0, kp1)
    early = max(1, heads - 3)
    share = -(-len(units) // early)
    done = 0
    for h in range(heads):
        fold_keys(kps[h % 2], taps_ref, rhs, h, h // per, dims)
        if h < early:
            for unit in units[h * share : (h + 1) * share]:
                unit()
        else:
            for _ in range(2):
                if done < h:
                    finish_head(done)
                    done += 1
        both = dot_nt(kps[h % 2][...], qcat_ref[h])
        sc[h] = both[:rows] + both[rows:]
    for h in range(done, heads):
        finish_head(h)


def first_positions(dims, place, qcat_ref, taps_ref, kv_ref, corner_ref, state_in, state):
    rows, heads, kv, width, q_taps, k_taps = dims
    per = heads // kv
    reach = q_taps - 1 + k_taps // 2
    key_id = lax.broadcasted_iota(jnp.int32, (HALO, rows), 0)
    row_id = place * rows + lax.broadcasted_iota(jnp.int32, (HALO, rows), 1)
    for g in range(kv):
        window = first_window(kv_ref, g, width)
        at = slice(g * width, (g + 1) * width)
        for h in range(g * per, (g + 1) * per):
            both = dot_nt(first_folded(taps_ref, window, h, q_taps), qcat_ref[h])
            scores = both[:HALO] + both[HALO:]
            exact = jnp.concatenate([corner_ref[h, HALO:]] * (rows // LANES), 1)
            scores = jnp.where(row_id - key_id < reach, exact, scores)
            scores = jnp.where(key_id <= row_id, scores, NEG_FILL)
            update(scores, kv_ref.at[rows : rows + HALO], at, h, *state_in, *state)


def needed(routes, step, count):
    reads = {routes[at][step - i] for at in range(step, count) for i in range(2)}
    if step == count - 1:
        reads |= {routes[at][at] for at in range(step)}
    return sorted(reads)


def step_kernel(dims, step, count, routes, qcat_ref, taps_ref, corner_ref, m_in, l_in, acc_in, *rest):
    rows, heads, kv, width, q_taps, k_taps = dims
    per = heads // kv
    reach = q_taps - 1 + k_taps // 2
    final = step == count - 1
    messages = dict(zip(needed(routes, step, count), rest[:-9]))
    m_ref, l_ref, acc_ref, rhs, kp0, kp1, sc0, sc1, vals = rest[-9:]
    place = lax.axis_index("ctx")
    states = (m_in, l_in, acc_in), (m_ref, l_ref, acc_ref)

    @pl.when(place >= step)
    def _():
        pairs = [(routes[at][step], routes[at][step - 1]) for at in range(step, count)]
        for pair in sorted(set(pairs)):
            here = [step + i for i, other in enumerate(pairs) if other == pair]

            def load(body=messages[pair[0]], after=messages[pair[1]]):
                fill_windows(rhs, body, after, dims)
                fill_values(vals, body, after, dims)

            if len(here) == len(pairs):
                load()
            else:
                pl.when(functools.reduce(jnp.logical_or, [place == at for at in here]))(load)
        body = messages[routes[count - 1][step]]
        if final:
            vals[rows:] = body[rows : rows + HALO]
        key_id = lax.broadcasted_iota(jnp.int32, (2 * HALO, LANES), 0) - HALO
        row_id = lax.broadcasted_iota(jnp.int32, (2 * HALO, LANES), 1)
        kps, scs = (kp0, kp1), (sc0, sc1)

        def fold(h):
            fold_keys(kps[h % 2], taps_ref, rhs, h, h // per, dims)
            if final:
                window = first_window(body, h // per, width)
                kps[h % 2][2 * rows :] = first_folded(taps_ref, window, h, q_taps)

        fold(0)
        for h in range(heads):
            g = h // per
            sc = scs[h % 2]
            both = dot_nt(kps[h % 2][...], qcat_ref[h])
            sc[:rows] = both[:rows] + both[rows : 2 * rows]
            if final:
                sc[rows:] = both[2 * rows : 2 * rows + HALO] + both[2 * rows + HALO :]
            if h + 1 < heads:
                fold(h + 1)
            if step == 1:
                at = slice(rows - 2 * HALO, rows)
                patch = sc[at, :LANES]
                patch = jnp.where(row_id - key_id < reach, corner_ref[h], patch)
                sc[at, :LANES] = jnp.where(key_id <= row_id, patch, NEG_FILL)
            at = slice(g * width, (g + 1) * width)
            update(sc[...], vals, at, h, *states[0], *states[1])

    if final:
        for at in range(step):
            @pl.when(place == at)
            def _(at=at):
                first_positions(
                    dims, place, qcat_ref, taps_ref, messages[routes[at][at]], corner_ref, *states
                )


def final_kernel(dims, l_ref, acc_ref, gain_ref, mix_ref, bounds_ref, o_ref):
    rows, heads, kv, width, _, _ = dims
    per = heads // kv
    row_pos = lax.axis_index("ctx") * rows + lax.broadcasted_iota(jnp.int32, (rows, 1), 0)
    live = (row_pos >= bounds_ref[0]) & (row_pos < bounds_ref[1])
    for g in range(kv):
        probs = [acc_ref[h] * (1.0 / l_ref[h : h + 1, :]) for h in range(g * per, (g + 1) * per)]
        for a in range(per):
            blended = mix_ref[g, a, 0] * probs[0]
            for b in range(1, per):
                blended = blended + mix_ref[g, a, b] * probs[b]
            mean_sq = jnp.mean(blended * blended, axis=0, keepdims=True)
            normed = (blended * lax.rsqrt(mean_sq + EPSILON)).T
            h = g * per + a
            normed = normed * gain_ref[:, h * width : (h + 1) * width]
            o_ref[:, h * width : (h + 1) * width] = jnp.where(live, normed, 0.0).astype(jnp.bfloat16)


VMEM = pl.BlockSpec(memory_space=pltpu.VMEM)
SMEM = pl.BlockSpec(memory_space=pltpu.SMEM)
HBM = pl.BlockSpec(memory_space=pltpu.HBM)


def send(value, pairs):
    return lax.ppermute(value, "ctx", pairs)


def spread_messages(own, count):
    if count == 4:
        ahead = send(own, [(0, 2), (2, 3)])
        near = send(own, [(0, 1), (1, 2)])
        skip = send(own, [(1, 3)])
        return [own, ahead, skip, near], [[0], [0, 3], [0, 3, 1], [0, 1, 2, 4]]
    first = send(own, [(at, at + 1) for at in range(count - 1)])
    return [own, first], [list(range(at + 1)) for at in range(count)]


def forward_messages(messages, marker, count):
    if count == 4:
        ahead, marker = lax.optimization_barrier((messages[1], marker))
        return [*messages, send(ahead, [(2, 3)])], marker
    for step in range(2, count):
        pairs = [(at, at + 1) for at in range(step - 1, count - 1)]
        messages = [*messages, send(messages[-1], pairs)]
    return messages, marker


def cost(flops):
    return pl.CostEstimate(flops=flops, bytes_accessed=2**20, transcendentals=0)


def attend(queries, keys, values, conv_kernel, head_mix, norm_gain, bounds):
    rows = queries.shape[0]
    kv, _ = head_mix.shape[:2]
    width = keys.shape[1] // kv
    heads, q_taps, k_taps = conv_kernel.shape
    count = lax.axis_size("ctx")
    dims = (rows, heads, kv, width, q_taps, k_taps)
    f32, bf16 = jnp.float32, jnp.bfloat16
    params = pltpu.CompilerParams(vmem_limit_bytes=28 * 2**20)

    columns = kv * width
    taps_in = conv_kernel.transpose(1, 0, 2)
    queries, keys, values, taps_in = (
        pltpu.with_memory_space_constraint(value, pltpu.HBM)
        for value in (queries, keys, values, taps_in)
    )
    edges, own = pl.pallas_call(
        functools.partial(pack_kernel, dims),
        name="pack",
        out_shape=(
            pltpu.VMEM((HALO, heads * width + columns), bf16),
            pltpu.VMEM((2 * rows, columns), bf16),
        ),
        in_specs=[HBM, HBM, HBM],
        out_specs=(VMEM, VMEM),
        scratch_shapes=[pltpu.SemaphoreType.DMA((4,))],
        compiler_params=params,
    )(queries, keys, values)
    edges = send(edges, [(at, at + 1) for at in range(count - 1)])
    messages, routes = spread_messages(own, count)

    def scratch(extra):
        return [
            pltpu.VMEM((kv, 2 * LANES, rows // BLOCK * width), bf16),
            pltpu.VMEM((2 * (rows + extra), q_taps * width), bf16),
            pltpu.VMEM((2 * (rows + extra), q_taps * width), bf16),
            pltpu.VMEM((rows + extra, rows), f32),
            pltpu.VMEM((rows + extra, rows), f32),
            pltpu.VMEM((rows + extra, columns), bf16),
        ]

    state = [
        pltpu.VMEM((heads, rows), f32),
        pltpu.VMEM((heads, rows), f32),
        pltpu.VMEM((heads, width, rows), f32),
    ]
    deltas = q_taps + k_taps - 1
    qcat, taps, top, total, acc, corner = pl.pallas_call(
        functools.partial(own_kernel, dims),
        name="own_shard",
        out_shape=(
            pltpu.VMEM((heads, rows, q_taps * width), bf16),
            pltpu.VMEM((heads, q_taps * BLOCK, 2 * LANES), bf16),
            *state,
            pltpu.VMEM((heads, 2 * HALO, LANES), f32),
        ),
        in_specs=[HBM, VMEM, VMEM, HBM],
        out_specs=(VMEM,) * 6,
        scratch_shapes=[
            pltpu.VMEM((rows, heads * width), bf16),
            pltpu.VMEM((q_taps, heads, k_taps), f32),
            pltpu.VMEM((q_taps * 16, LANES), f32),
            pltpu.VMEM((rows + HALO, width), f32),
            *scratch(0)[:3],
            pltpu.VMEM((heads, rows, rows), f32),
            pltpu.VMEM((rows, columns), bf16),
            pltpu.VMEM((deltas, rows + HALO + 16, LANES), f32),
            pltpu.VMEM((rows + 2 * HALO, LANES), f32),
            pltpu.VMEM((rows + HALO, LANES), f32),
            pltpu.SemaphoreType.DMA((2,)),
        ],
        compiler_params=params,
        cost_estimate=cost(6 * 10**9),
    )(queries, own, edges, taps_in)
    messages, corner = forward_messages(messages, corner, count)
    for step in range(1, count):
        reads = needed(routes, step, count)
        top, total, acc = pl.pallas_call(
            functools.partial(step_kernel, dims, step, count, routes),
            name="shard_step",
            out_shape=tuple(state),
            in_specs=[VMEM] * (6 + len(reads)),
            out_specs=(VMEM,) * 3,
            scratch_shapes=scratch(HALO if step == count - 1 else 0),
            input_output_aliases={3: 0, 4: 1, 5: 2},
            compiler_params=params,
            cost_estimate=cost(5 * 10**9),
        )(qcat, taps, corner, top, total, acc, *(messages[i] for i in reads))
    return pl.pallas_call(
        functools.partial(final_kernel, dims),
        name="finish",
        out_shape=jax.ShapeDtypeStruct((rows, heads * width), bf16),
        in_specs=[VMEM] * 3 + [SMEM] * 2,
        out_specs=VMEM,
        compiler_params=params,
    )(total, acc, norm_gain.reshape(1, -1), head_mix, bounds)


def solution(mesh):
    return jax.shard_map(
        attend,
        mesh=mesh,
        in_specs=(
            P(("groups", "ctx"), "heads"),
            P(("groups", "ctx"), "heads"),
            P(("groups", "ctx"), "heads"),
            P("heads", None, None),
            P("heads", None, None),
            P("heads"),
            P("groups"),
        ),
        out_specs=P(("groups", "ctx"), "heads"),
        check_vma=False,
    )
```

profile of v0, /device:TPU:20, one launch (start us, length us, event | category | flops | bytes accessed | tf_op | source)
XLA Modules:
  0.0 41.6 jit_solution(10219232641283660846)
XLA Ops:
  0.0 1.0 %pack.1 = (bf16[16,1280]{1,0:T(8,128)(2,1)S(1)}, bf16[512,256]{1,0:T(8,128)(2,1)S(1)}) custom-call(bf16[256,1024]{1,0:T(8,128)(2,1)} %q_hbm.3, bf16[256,256]{1,0:T(8,128)(2,1)} %k_hbm.1, bf16[256,256]{1,0:T(8,128)(2,1)} %v_hbm.1), custom_call_target="tpu_custom_call" | custom-call | tf_op jit(solution)/shard_map/pack/pallas_call | solution.py:449
  1.0 3.5 %collective-permute-start = (bf16[16,1280]{1,0:T(8,128)(2,1)S(1)}, bf16[16,1280]{1,0:T(8,128)(2,1)S(1)}, u32[]{:S(2)}, u32[]{:S(2)}) collective-permute-start(bf16[16,1280]{1,0:T(8,128)(2,1)S(1)} %get-tuple-element.24), channel_id=1, source_target_pairs={{0,4},{4,8},{8,12},{1,5},{5,9},{9,13},{2,6},{6,10},{10,14},{3,7},{... | collective-permute-start | bytes 122888 | tf_op jit(solution)/shard_map/ppermute | solution.py:406
  4.5 0.7 %collective-permute-start.3 = (bf16[512,256]{1,0:T(8,128)(2,1)S(1)}, bf16[512,256]{1,0:T(8,128)(2,1)S(1)}, u32[]{:S(2)}, u32[]{:S(2)}) collective-permute-start(bf16[512,256]{1,0:T(8,128)(2,1)S(1)} %get-tuple-element.23.kv_ref.rest_0_), channel_id=1, source_target_pairs={{4,12},{5,13},{6,14},{7,15},{20,28},{21,29},{22,30},{23,31}} | collective-permute-start | bytes 786440 | tf_op jit(solution)/shard_map/ppermute | solution.py:406
  5.2 1.3 %collective-permute-start.2 = (bf16[512,256]{1,0:T(8,128)(2,1)S(1)}, bf16[512,256]{1,0:T(8,128)(2,1)S(1)}, u32[]{:S(2)}, u32[]{:S(2)}) collective-permute-start(bf16[512,256]{1,0:T(8,128)(2,1)S(1)} %get-tuple-element.23.kv_ref.rest_0_), channel_id=1, source_target_pairs={{0,4},{4,8},{1,5},{5,9},{2,6},{6,10},{3,7},{7,11},{16,20},{20,24},... | collective-permute-start | bytes 786440 | tf_op jit(solution)/shard_map/ppermute | solution.py:406
  6.5 1.9 %collective-permute-start.1 = (bf16[512,256]{1,0:T(8,128)(2,1)S(1)}, bf16[512,256]{1,0:T(8,128)(2,1)S(1)}, u32[]{:S(2)}, u32[]{:S(2)}) collective-permute-start(bf16[512,256]{1,0:T(8,128)(2,1)S(1)} %get-tuple-element.23.kv_ref.rest_0_), channel_id=1, source_target_pairs={{0,8},{8,12},{1,9},{9,13},{2,10},{10,14},{3,11},{11,15},{16,24},{2... | collective-permute-start | bytes 786440 | tf_op jit(solution)/shard_map/ppermute | solution.py:406
  8.5 0.0 collective-permute-done.e_ref
  8.5 6.7 %own_shard.1 = (bf16[8,256,768]{2,1,0:T(8,128)(2,1)S(1)}, bf16[8,384,256]{2,1,0:T(8,128)(2,1)S(1)}, f32[8,256]{1,0:T(8,128)S(1)}, f32[8,256]{1,0:T(8,128)S(1)}, ...) custom-call(bf16[256,1024]{1,0:T(8,128)(2,1)} %q_hbm.3, bf16[512,256]{1,0:T(8,128)(2,1)S(1)} %get-tuple-element.23.kv_ref.rest_0_, ...), custom_call_target="tpu_custom_call" | custom-call | flops 6000000000 | bytes 1048576 | tf_op jit(solution)/shard_map/own_shard/pallas_call | solution.py:480
  15.2 7.0 %collective-permute-done.1.rest_1_.rest_0_ = bf16[512,256]{1,0:T(8,128)(2,1)S(1)} collective-permute-done((bf16[512,256]{1,0:T(8,128)(2,1)S(1)}, bf16[512,256]{1,0:T(8,128)(2,1)S(1)}, u32[]{:S(2)}, u32[]{:S(2)}) %collective-permute-start.1) | collective-permute-done | bytes 262176 | tf_op jit(solution)/shard_map/ppermute | solution.py:406
  22.1 1.3 %collective-permute-start.4 = (bf16[512,256]{1,0:T(8,128)(2,1)S(1)}, bf16[512,256]{1,0:T(8,128)(2,1)S(1)}, u32[]{:S(2)}, u32[]{:S(2)}) collective-permute-start(bf16[512,256]{1,0:T(8,128)(2,1)S(1)} %collective-permute-done.1.rest_1_.rest_0_), channel_id=1, source_target_pairs={{8,12},{9,13},{10,14},{11,15},{24,28},{25,29},{26,30},{27,31}} | collective-permute-start | bytes 786440 | tf_op jit(solution)/shard_map/ppermute | solution.py:406
  23.4 1.1 %collective-permute-done.2.rest_2_.rest_3_ = bf16[512,256]{1,0:T(8,128)(2,1)S(1)} collective-permute-done((bf16[512,256]{1,0:T(8,128)(2,1)S(1)}, bf16[512,256]{1,0:T(8,128)(2,1)S(1)}, u32[]{:S(2)}, u32[]{:S(2)}) %collective-permute-start.2) | collective-permute-done | bytes 262176 | tf_op jit(solution)/shard_map/ppermute | solution.py:406
  24.6 5.3 %shard_step.3 = (f32[8,256]{1,0:T(8,128)S(1)}, f32[8,256]{1,0:T(8,128)S(1)}, f32[8,128,256]{2,1,0:T(8,128)S(1)}) custom-call(bf16[8,256,768]{2,1,0:T(8,128)(2,1)S(1)} %get-tuple-element.25.qcat_ref, bf16[8,384,256]{2,1,0:T(8,128)(2,1)S(1)} %get-tuple-element.26.taps_ref, ...), custom_call_target="tpu_custom_call", output_to_operand_aliasing={{0}: (3, {}), {1}: (4, {}), {2}: (5, {})} | custom-call | flops 5000000000 | bytes 1048576 | tf_op jit(solution)/shard_map/shard_step/pallas_call | solution.py:510
  29.9 0.0 collective-permute-done.3.rest_1_.rest_2_
  29.9 5.7 %shard_step.4 = (f32[8,256]{1,0:T(8,128)S(1)}, f32[8,256]{1,0:T(8,128)S(1)}, f32[8,128,256]{2,1,0:T(8,128)S(1)}) custom-call(bf16[8,256,768]{2,1,0:T(8,128)(2,1)S(1)} %get-tuple-element.25.qcat_ref, bf16[8,384,256]{2,1,0:T(8,128)(2,1)S(1)} %get-tuple-element.26.taps_ref, ...), custom_call_target="tpu_custom_call", output_to_operand_aliasing={{0}: (3, {}), {1}: (4, {}), {2}: (5, {})} | custom-call | flops 5000000000 | bytes 1048576 | tf_op jit(solution)/shard_map/shard_step/pallas_call | solution.py:510
  35.6 0.0 collective-permute-done.4.rest_4_
  35.6 0.0 copy-start
  35.7 0.0 copy-start.1
  35.7 0.0 copy-start.2
  35.7 3.8 %shard_step.5 = (f32[8,256]{1,0:T(8,128)S(1)}, f32[8,256]{1,0:T(8,128)S(1)}, f32[8,128,256]{2,1,0:T(8,128)S(1)}) custom-call(bf16[8,256,768]{2,1,0:T(8,128)(2,1)S(1)} %get-tuple-element.25.qcat_ref, bf16[8,384,256]{2,1,0:T(8,128)(2,1)S(1)} %get-tuple-element.26.taps_ref, ...), custom_call_target="tpu_custom_call", output_to_operand_aliasing={{0}: (3, {}), {1}: (4, {}), {2}: (5, {})} | custom-call | flops 5000000000 | bytes 1048576 | tf_op jit(solution)/shard_map/shard_step/pallas_call | solution.py:510
  39.5 0.0 copy-done
  39.5 0.0 copy-done.1
  39.5 0.0 copy-done.2
  39.5 2.1 %finish.1 = bf16[256,1024]{1,0:T(8,128)(2,1)} custom-call(f32[8,256]{1,0:T(8,128)S(1)} %get-tuple-element.39.l_ref, f32[8,128,256]{2,1,0:T(8,128)S(1)} %get-tuple-element.40.acc_ref, f32[1,1024]{1,0:T(1,128)S(1)} %bitcast.2, f32[2,4,4]{2,1,0:T(4,128)S(1)} %copy-done.1, s32[2]{0:T(128)S(1)} %copy-done.2), custom_call_target="tpu_custom_call" | custom-call | tf_op jit(solution)/shard_map/finish/pallas_call | solution.py:521
Async XLA Ops:
  1.0 7.4 %collective-permute-start = (bf16[16,1280]{1,0:T(8,128)(2,1)S(1)}, bf16[16,1280]{1,0:T(8,128)(2,1)S(1)}, u32[]{:S(2)}, u32[]{:S(2)}) collective-permute-start(bf16[16,1280]{1,0:T(8,128)(2,1)S(1)} %get-tuple-element.24), channel_id=1, source_target_pairs={{0,4},{4,8},{8,12},{1,5},{5,9},{9,13},{2,6},{6,10},{10,14},{3,7},{... | collective-permute-start | bytes 122888 | tf_op jit(solution)/shard_map/ppermute | solution.py:406
  4.5 25.4 %collective-permute-start.3 = (bf16[512,256]{1,0:T(8,128)(2,1)S(1)}, bf16[512,256]{1,0:T(8,128)(2,1)S(1)}, u32[]{:S(2)}, u32[]{:S(2)}) collective-permute-start(bf16[512,256]{1,0:T(8,128)(2,1)S(1)} %get-tuple-element.23.kv_ref.rest_0_), channel_id=1, source_target_pairs={{4,12},{5,13},{6,14},{7,15},{20,28},{21,29},{22,30},{23,31}} | collective-permute-start | bytes 786440 | tf_op jit(solution)/shard_map/ppermute | solution.py:406
  5.2 19.4 %collective-permute-start.2 = (bf16[512,256]{1,0:T(8,128)(2,1)S(1)}, bf16[512,256]{1,0:T(8,128)(2,1)S(1)}, u32[]{:S(2)}, u32[]{:S(2)}) collective-permute-start(bf16[512,256]{1,0:T(8,128)(2,1)S(1)} %get-tuple-element.23.kv_ref.rest_0_), channel_id=1, source_target_pairs={{0,4},{4,8},{1,5},{5,9},{2,6},{6,10},{3,7},{7,11},{16,20},{20,24},... | collective-permute-start | bytes 786440 | tf_op jit(solution)/shard_map/ppermute | solution.py:406
  6.5 15.6 %collective-permute-start.1 = (bf16[512,256]{1,0:T(8,128)(2,1)S(1)}, bf16[512,256]{1,0:T(8,128)(2,1)S(1)}, u32[]{:S(2)}, u32[]{:S(2)}) collective-permute-start(bf16[512,256]{1,0:T(8,128)(2,1)S(1)} %get-tuple-element.23.kv_ref.rest_0_), channel_id=1, source_target_pairs={{0,8},{8,12},{1,9},{9,13},{2,10},{10,14},{3,11},{11,15},{16,24},{2... | collective-permute-start | bytes 786440 | tf_op jit(solution)/shard_map/ppermute | solution.py:406
  22.1 13.5 %collective-permute-start.4 = (bf16[512,256]{1,0:T(8,128)(2,1)S(1)}, bf16[512,256]{1,0:T(8,128)(2,1)S(1)}, u32[]{:S(2)}, u32[]{:S(2)}) collective-permute-start(bf16[512,256]{1,0:T(8,128)(2,1)S(1)} %collective-permute-done.1.rest_1_.rest_0_), channel_id=1, source_target_pairs={{8,12},{9,13},{10,14},{11,15},{24,28},{25,29},{26,30},{27,31}} | collective-permute-start | bytes 786440 | tf_op jit(solution)/shard_map/ppermute | solution.py:406
  35.6 3.9 %copy-start = (f32[1024]{0:T(1024)S(1)}, f32[1024]{0:T(1024)}, u32[]{:S(2)}) copy-start(f32[1024]{0:T(1024)} %param.12) | copy-start | bytes 12292
  35.7 3.9 %copy-start.1 = (f32[2,4,4]{2,1,0:T(4,128)S(1)}, f32[2,4,4]{2,1,0:T(4,128)}, u32[]{:S(2)}) copy-start(f32[2,4,4]{2,1,0:T(4,128)} %mix_ref.1) | copy-start | bytes 388
  35.7 3.9 %copy-start.2 = (s32[2]{0:T(128)S(1)}, s32[2]{0:T(128)}, u32[]{:S(2)}) copy-start(s32[2]{0:T(128)} %bounds_ref.1) | copy-start | bytes 28
where the time goes:
time: 41.8 us; the launch traced here: 41.6 us
  Pallas kernels  24.7 us (59%)
  starting transfers between devices  8.67 us (21%)
  waiting for transfers between devices  8.13 us (19%)
    pallas_call x3, Pallas kernels, attend(): pl.pallas_call(functools.partial(step_kernel, dims, step, count, routes),...  14.9 us
    ppermute x5, starting transfers between devices, send(): return lax.ppermute(value, 'ctx', pairs)  8.67 us
    ppermute x5, waiting for transfers between devices, send(): return lax.ppermute(value, 'ctx', pairs)  8.13 us
    pallas_call x1, Pallas kernels, attend(): pl.pallas_call(functools.partial(own_kernel, dims), name='own_shard', out...  6.68 us
    pallas_call x1, Pallas kernels, attend(): pl.pallas_call(functools.partial(final_kernel, dims), name='finish', out_...  2.08 us
    pallas_call x1, Pallas kernels, attend(): pl.pallas_call(functools.partial(pack_kernel, dims), name='pack', out_sha...  1.04 us
  transfers between devices with their start and end apart: 5, of which 2 were waited for; matrix products, arithmetic and copies ran while one was open for 0% of the time, Pallas kernels for 43%

commit v1 on v0

--- a/solution.py
+++ b/solution.py
@@ -59,13 +59,16 @@
 
 def fold_keys(kp, taps, rhs, h, g, dims):
     rows, _, _, width, q_taps, _ = dims
-    for a in range(q_taps):
-        out = dot(taps[h, a * BLOCK : (a + 1) * BLOCK], rhs[g])
-        for blk in range(rows // BLOCK):
-            high, low = split(out[:, blk * width : (blk + 1) * width])
-            at = blk * BLOCK
-            kp[at : at + BLOCK, a * width : (a + 1) * width] = high
-            kp[rows + at : rows + at + BLOCK, a * width : (a + 1) * width] = low
+    pair = 2 * width
+    for half in range(rows // BLOCK // 2):
+        out = dot(taps[h], rhs[g, :, half * pair : (half + 1) * pair])
+        for a in range(q_taps):
+            for i in range(2):
+                piece = out[a * BLOCK : (a + 1) * BLOCK, i * width : (i + 1) * width]
+                high, low = split(piece)
+                at = (2 * half + i) * BLOCK
+                kp[at : at + BLOCK, a * width : (a + 1) * width] = high
+                kp[rows + at : rows + at + BLOCK, a * width : (a + 1) * width] = low
 
 
 def fill_values(vals, body, after, dims):
@@ -408,21 +411,22 @@
 
 def spread_messages(own, count):
     if count == 4:
-        ahead = send(own, [(0, 2), (2, 3)])
-        near = send(own, [(0, 1), (1, 2)])
-        skip = send(own, [(1, 3)])
-        return [own, ahead, skip, near], [[0], [0, 3], [0, 3, 1], [0, 1, 2, 4]]
+        first = send(own, [(0, 1), (1, 2), (2, 3)])
+        second = send(own, [(0, 2)])
+        return [own, first, second], [[0], [0, 1], [0, 1, 2], [0, 1, 3, 4]]
     first = send(own, [(at, at + 1) for at in range(count - 1)])
     return [own, first], [list(range(at + 1)) for at in range(count)]
 
 
-def forward_messages(messages, marker, count):
-    if count == 4:
-        ahead, marker = lax.optimization_barrier((messages[1], marker))
-        return [*messages, send(ahead, [(2, 3)])], marker
-    for step in range(2, count):
-        pairs = [(at, at + 1) for at in range(step - 1, count - 1)]
-        messages = [*messages, send(messages[-1], pairs)]
+def forward_messages(messages, marker, count, stage):
+    if count != 4:
+        chain = range(2, count) if stage == 0 else ()
+        for step in chain:
+            pairs = [(at, at + 1) for at in range(step - 1, count - 1)]
+            messages = [*messages, send(messages[-1], pairs)]
+    elif stage < 2:
+        source, marker = lax.optimization_barrier((messages[stage + 1], marker))
+        messages = [*messages, send(source, [(2, 3)])]
     return messages, marker
 
 
@@ -504,7 +508,7 @@
         compiler_params=params,
         cost_estimate=cost(6 * 10**9),
     )(queries, own, edges, taps_in)
-    messages, corner = forward_messages(messages, corner, count)
+    messages, corner = forward_messages(messages, corner, count, 0)
     for step in range(1, count):
         reads = needed(routes, step, count)
         top, total, acc = pl.pallas_call(
@@ -518,6 +522,7 @@
             compiler_params=params,
             cost_estimate=cost(5 * 10**9),
         )(qcat, taps, corner, top, total, acc, *(messages[i] for i in reads))
+        messages, top = forward_messages(messages, top, count, step)
     return pl.pallas_call(
         functools.partial(final_kernel, dims),
         name="finish",

time: 41.8 us -> 44.6 us (1.067)
  the two profiles are of different devices: /device:TPU:20 before, /device:TPU:28 now
where the time goes in v1:
time: 44.6 us; the launch traced here: 44.4 us
  Pallas kernels  27.3 us (61%)
  waiting for transfers between devices  11.2 us (25%)
  starting transfers between devices  5.83 us (13%)
    pallas_call x3, Pallas kernels, attend(): pl.pallas_call(functools.partial(step_kernel, dims, step, count, routes),...  18.1 us
    ppermute x5, waiting for transfers between devices, send(): return lax.ppermute(value, 'ctx', pairs)  11.2 us
    pallas_call x1, Pallas kernels, attend(): pl.pallas_call(functools.partial(own_kernel, dims), name='own_shard', out...  6.02 us
    ppermute x5, starting transfers between devices, send(): return lax.ppermute(value, 'ctx', pairs)  5.83 us
    pallas_call x1, Pallas kernels, attend(): pl.pallas_call(functools.partial(final_kernel, dims), name='finish', out_...  2.08 us
    pallas_call x1, Pallas kernels, attend(): pl.pallas_call(functools.partial(pack_kernel, dims), name='pack', out_sha...  1.04 us
  transfers between devices with their start and end apart: 5, of which 4 were waited for; matrix products, arithmetic and copies ran while one was open for 0% of the time, Pallas kernels for 40%

profile of v1, /device:TPU:28, one launch (start us, length us, event | category | flops | bytes accessed | tf_op | source)
XLA Modules:
  0.0 44.4 jit_solution(17116331956052173502)
XLA Ops:
  0.0 1.0 %pack.1 = (bf16[16,1280]{1,0:T(8,128)(2,1)S(1)}, bf16[512,256]{1,0:T(8,128)(2,1)S(1)}) custom-call(bf16[256,1024]{1,0:T(8,128)(2,1)} %q_hbm.3, bf16[256,256]{1,0:T(8,128)(2,1)} %k_hbm.1, bf16[256,256]{1,0:T(8,128)(2,1)} %v_hbm.1), custom_call_target="tpu_custom_call" | custom-call | tf_op jit(solution)/shard_map/pack/pallas_call | solution.py:453
  1.0 1.3 %collective-permute-start = (bf16[16,1280]{1,0:T(8,128)(2,1)S(1)}, bf16[16,1280]{1,0:T(8,128)(2,1)S(1)}, u32[]{:S(2)}, u32[]{:S(2)}) collective-permute-start(bf16[16,1280]{1,0:T(8,128)(2,1)S(1)} %get-tuple-element.26), channel_id=1, source_target_pairs={{0,4},{4,8},{8,12},{1,5},{5,9},{9,13},{2,6},{6,10},{10,14},{3,7},{... | collective-permute-start | bytes 122888 | tf_op jit(solution)/shard_map/ppermute | solution.py:409
  2.3 0.7 %collective-permute-start.2 = (bf16[512,256]{1,0:T(8,128)(2,1)S(1)}, bf16[512,256]{1,0:T(8,128)(2,1)S(1)}, u32[]{:S(2)}, u32[]{:S(2)}) collective-permute-start(bf16[512,256]{1,0:T(8,128)(2,1)S(1)} %get-tuple-element.25.kv_ref.rest_0_), channel_id=1, source_target_pairs={{0,8},{1,9},{2,10},{3,11},{16,24},{17,25},{18,26},{19,27}} | collective-permute-start | bytes 786440 | tf_op jit(solution)/shard_map/ppermute | solution.py:409
  3.0 1.3 %collective-permute-start.1 = (bf16[512,256]{1,0:T(8,128)(2,1)S(1)}, bf16[512,256]{1,0:T(8,128)(2,1)S(1)}, u32[]{:S(2)}, u32[]{:S(2)}) collective-permute-start(bf16[512,256]{1,0:T(8,128)(2,1)S(1)} %get-tuple-element.25.kv_ref.rest_0_), channel_id=1, source_target_pairs={{0,4},{4,8},{8,12},{1,5},{5,9},{9,13},{2,6},{6,10},{10,14},{3,7},{... | collective-permute-start | bytes 786440 | tf_op jit(solution)/shard_map/ppermute | solution.py:409
  4.3 2.6 %collective-permute-done.e_ref = bf16[16,1280]{1,0:T(8,128)(2,1)S(1)} collective-permute-done((bf16[16,1280]{1,0:T(8,128)(2,1)S(1)}, bf16[16,1280]{1,0:T(8,128)(2,1)S(1)}, u32[]{:S(2)}, u32[]{:S(2)}) %collective-permute-start) | collective-permute-done | bytes 40992 | tf_op jit(solution)/shard_map/ppermute | solution.py:409
  6.9 6.0 %own_shard.1 = (bf16[8,256,768]{2,1,0:T(8,128)(2,1)S(1)}, bf16[8,384,256]{2,1,0:T(8,128)(2,1)S(1)}, f32[8,256]{1,0:T(8,128)S(1)}, f32[8,256]{1,0:T(8,128)S(1)}, ...) custom-call(bf16[256,1024]{1,0:T(8,128)(2,1)} %q_hbm.3, bf16[512,256]{1,0:T(8,128)(2,1)S(1)} %get-tuple-element.25.kv_ref.rest_0_, ...), custom_call_target="tpu_custom_call" | custom-call | flops 6000000000 | bytes 1048576 | tf_op jit(solution)/shard_map/own_shard/pallas_call | solution.py:484
  13.0 1.2 %collective-permute-done.1.rest_1_.rest_0_ = bf16[512,256]{1,0:T(8,128)(2,1)S(1)} collective-permute-done((bf16[512,256]{1,0:T(8,128)(2,1)S(1)}, bf16[512,256]{1,0:T(8,128)(2,1)S(1)}, u32[]{:S(2)}, u32[]{:S(2)}) %collective-permute-start.1) | collective-permute-done | bytes 262176 | tf_op jit(solution)/shard_map/ppermute | solution.py:409
  14.2 1.3 %collective-permute-start.3 = (bf16[512,256]{1,0:T(8,128)(2,1)S(1)}, bf16[512,256]{1,0:T(8,128)(2,1)S(1)}, u32[]{:S(2)}, u32[]{:S(2)}) collective-permute-start(bf16[512,256]{1,0:T(8,128)(2,1)S(1)} %collective-permute-done.1.rest_1_.rest_0_), channel_id=1, source_target_pairs={{8,12},{9,13},{10,14},{11,15},{24,28},{25,29},{26,30},{27,31}} | collective-permute-start | bytes 786440 | tf_op jit(solution)/shard_map/ppermute | solution.py:409
  15.5 5.7 %shard_step.3 = (f32[8,256]{1,0:T(8,128)S(1)}, f32[8,256]{1,0:T(8,128)S(1)}, f32[8,128,256]{2,1,0:T(8,128)S(1)}) custom-call(bf16[8,256,768]{2,1,0:T(8,128)(2,1)S(1)} %get-tuple-element.27.qcat_ref, bf16[8,384,256]{2,1,0:T(8,128)(2,1)S(1)} %get-tuple-element.28.taps_ref, ...), custom_call_target="tpu_custom_call", output_to_operand_aliasing={{0}: (3, {}), {1}: (4, {}), {2}: (5, {})} | custom-call | flops 5000000000 | bytes 1048576 | tf_op jit(solution)/shard_map/shard_step/pallas_call | solution.py:514
  21.2 0.0 collective-permute-done.2.rest_1_.rest_2_
  21.2 1.3 %collective-permute-start.4 = (bf16[512,256]{1,0:T(8,128)(2,1)S(1)}, bf16[512,256]{1,0:T(8,128)(2,1)S(1)}, u32[]{:S(2)}, u32[]{:S(2)}) collective-permute-start(bf16[512,256]{1,0:T(8,128)(2,1)S(1)} %collective-permute-done.2.rest_1_.rest_2_), channel_id=1, source_target_pairs={{8,12},{9,13},{10,14},{11,15},{24,28},{25,29},{26,30},{27,31}} | collective-permute-start | bytes 786440 | tf_op jit(solution)/shard_map/ppermute | solution.py:409
  22.5 6.4 %collective-permute-done.3.rest_2_.rest_3_ = bf16[512,256]{1,0:T(8,128)(2,1)S(1)} collective-permute-done((bf16[512,256]{1,0:T(8,128)(2,1)S(1)}, bf16[512,256]{1,0:T(8,128)(2,1)S(1)}, u32[]{:S(2)}, u32[]{:S(2)}) %collective-permute-start.3) | collective-permute-done | bytes 262176 | tf_op jit(solution)/shard_map/ppermute | solution.py:409
  28.9 6.1 %shard_step.4 = (f32[8,256]{1,0:T(8,128)S(1)}, f32[8,256]{1,0:T(8,128)S(1)}, f32[8,128,256]{2,1,0:T(8,128)S(1)}) custom-call(bf16[8,256,768]{2,1,0:T(8,128)(2,1)S(1)} %get-tuple-element.27.qcat_ref, bf16[8,384,256]{2,1,0:T(8,128)(2,1)S(1)} %get-tuple-element.28.taps_ref, ...), custom_call_target="tpu_custom_call", output_to_operand_aliasing={{0}: (3, {}), {1}: (4, {}), {2}: (5, {})} | custom-call | flops 5000000000 | bytes 1048576 | tf_op jit(solution)/shard_map/shard_step/pallas_call | solution.py:514
  35.1 0.9 %collective-permute-done.4.rest_4_ = bf16[512,256]{1,0:T(8,128)(2,1)S(1)} collective-permute-done((bf16[512,256]{1,0:T(8,128)(2,1)S(1)}, bf16[512,256]{1,0:T(8,128)(2,1)S(1)}, u32[]{:S(2)}, u32[]{:S(2)}) %collective-permute-start.4) | collective-permute-done | bytes 262176 | tf_op jit(solution)/shard_map/ppermute | solution.py:409
  36.0 0.0 copy-start
  36.0 0.0 copy-start.1
  36.0 0.0 copy-start.2
  36.0 6.3 %shard_step.5 = (f32[8,256]{1,0:T(8,128)S(1)}, f32[8,256]{1,0:T(8,128)S(1)}, f32[8,128,256]{2,1,0:T(8,128)S(1)}) custom-call(bf16[8,256,768]{2,1,0:T(8,128)(2,1)S(1)} %get-tuple-element.27.qcat_ref, bf16[8,384,256]{2,1,0:T(8,128)(2,1)S(1)} %get-tuple-element.28.taps_ref, ...), custom_call_target="tpu_custom_call", output_to_operand_aliasing={{0}: (3, {}), {1}: (4, {}), {2}: (5, {})} | custom-call | flops 5000000000 | bytes 1048576 | tf_op jit(solution)/shard_map/shard_step/pallas_call | solution.py:514
  42.3 0.0 copy-done
  42.3 0.0 copy-done.1
  42.3 0.0 copy-done.2
  42.3 2.1 %finish.1 = bf16[256,1024]{1,0:T(8,128)(2,1)} custom-call(f32[8,256]{1,0:T(8,128)S(1)} %get-tuple-element.43.l_ref, f32[8,128,256]{2,1,0:T(8,128)S(1)} %get-tuple-element.44.acc_ref, f32[1,1024]{1,0:T(1,128)S(1)} %bitcast.2, f32[2,4,4]{2,1,0:T(4,128)S(1)} %copy-done.1, s32[2]{0:T(128)S(1)} %copy-done.2), custom_call_target="tpu_custom_call" | custom-call | tf_op jit(solution)/shard_map/finish/pallas_call | solution.py:526
Async XLA Ops:
  1.0 5.9 %collective-permute-start = (bf16[16,1280]{1,0:T(8,128)(2,1)S(1)}, bf16[16,1280]{1,0:T(8,128)(2,1)S(1)}, u32[]{:S(2)}, u32[]{:S(2)}) collective-permute-start(bf16[16,1280]{1,0:T(8,128)(2,1)S(1)} %get-tuple-element.26), channel_id=1, source_target_pairs={{0,4},{4,8},{8,12},{1,5},{5,9},{9,13},{2,6},{6,10},{10,14},{3,7},{... | collective-permute-start | bytes 122888 | tf_op jit(solution)/shard_map/ppermute | solution.py:409
  2.3 18.9 %collective-permute-start.2 = (bf16[512,256]{1,0:T(8,128)(2,1)S(1)}, bf16[512,256]{1,0:T(8,128)(2,1)S(1)}, u32[]{:S(2)}, u32[]{:S(2)}) collective-permute-start(bf16[512,256]{1,0:T(8,128)(2,1)S(1)} %get-tuple-element.25.kv_ref.rest_0_), channel_id=1, source_target_pairs={{0,8},{1,9},{2,10},{3,11},{16,24},{17,25},{18,26},{19,27}} | collective-permute-start | bytes 786440 | tf_op jit(solution)/shard_map/ppermute | solution.py:409
  3.0 11.2 %collective-permute-start.1 = (bf16[512,256]{1,0:T(8,128)(2,1)S(1)}, bf16[512,256]{1,0:T(8,128)(2,1)S(1)}, u32[]{:S(2)}, u32[]{:S(2)}) collective-permute-start(bf16[512,256]{1,0:T(8,128)(2,1)S(1)} %get-tuple-element.25.kv_ref.rest_0_), channel_id=1, source_target_pairs={{0,4},{4,8},{8,12},{1,5},{5,9},{9,13},{2,6},{6,10},{10,14},{3,7},{... | collective-permute-start | bytes 786440 | tf_op jit(solution)/shard_map/ppermute | solution.py:409
  14.2 14.7 %collective-permute-start.3 = (bf16[512,256]{1,0:T(8,128)(2,1)S(1)}, bf16[512,256]{1,0:T(8,128)(2,1)S(1)}, u32[]{:S(2)}, u32[]{:S(2)}) collective-permute-start(bf16[512,256]{1,0:T(8,128)(2,1)S(1)} %collective-permute-done.1.rest_1_.rest_0_), channel_id=1, source_target_pairs={{8,12},{9,13},{10,14},{11,15},{24,28},{25,29},{26,30},{27,31}} | collective-permute-start | bytes 786440 | tf_op jit(solution)/shard_map/ppermute | solution.py:409
  21.2 14.7 %collective-permute-start.4 = (bf16[512,256]{1,0:T(8,128)(2,1)S(1)}, bf16[512,256]{1,0:T(8,128)(2,1)S(1)}, u32[]{:S(2)}, u32[]{:S(2)}) collective-permute-start(bf16[512,256]{1,0:T(8,128)(2,1)S(1)} %collective-permute-done.2.rest_1_.rest_2_), channel_id=1, source_target_pairs={{8,12},{9,13},{10,14},{11,15},{24,28},{25,29},{26,30},{27,31}} | collective-permute-start | bytes 786440 | tf_op jit(solution)/shard_map/ppermute | solution.py:409
  36.0 6.3 %copy-start = (f32[1024]{0:T(1024)S(1)}, f32[1024]{0:T(1024)}, u32[]{:S(2)}) copy-start(f32[1024]{0:T(1024)} %param.12) | copy-start | bytes 12292
  36.0 6.3 %copy-start.1 = (f32[2,4,4]{2,1,0:T(4,128)S(1)}, f32[2,4,4]{2,1,0:T(4,128)}, u32[]{:S(2)}) copy-start(f32[2,4,4]{2,1,0:T(4,128)} %mix_ref.1) | copy-start | bytes 388
  36.0 6.3 %copy-start.2 = (s32[2]{0:T(128)S(1)}, s32[2]{0:T(128)}, u32[]{:S(2)}) copy-start(s32[2]{0:T(128)} %bounds_ref.1) | copy-start | bytes 28

commit v2 on v0

v2 whole, which is shorter than its diff:
```python
import functools

import jax
import jax.numpy as jnp
from jax import lax
from jax.experimental import pallas as pl
from jax.experimental.pallas import tpu as pltpu
from jax.sharding import PartitionSpec as P

EPSILON = 1e-06
NEG_FILL = -1e30
LANES = 128
HALO = 16
BLOCK = 64
SLOT = 16
FOLD_TAPS = 2


def dot(a, b):
    return jnp.dot(a, b, preferred_element_type=jnp.float32)


def dot_nt(a, b):
    return lax.dot_general(a, b, (((1,), (1,)), ((), ())), preferred_element_type=jnp.float32)


def dot_tn(a, b, precision=None):
    return lax.dot_general(
        a, b, (((0,), (0,)), ((), ())), precision=precision, preferred_element_type=jnp.float32
    )


def split(value):
    high = value.astype(jnp.bfloat16)
    return high, (value - high.astype(jnp.float32)).astype(jnp.bfloat16)


def slot_lane(h):
    return 2 * SLOT * (h % 4) + SLOT * (h // 4)


def fill_group(rhs, vals, g, body, after, dims):
    rows, _, _, width, _, _ = dims
    cols = slice(g * width, (g + 1) * width)
    for blk in range(rows // BLOCK):
        at = slice(blk * width, (blk + 1) * width)
        first, last = blk * BLOCK, blk * BLOCK + LANES
        if last <= rows:
            piece = body[first:last, cols]
        elif after is None:
            piece = jnp.concatenate(
                [body[first:rows, cols], jnp.zeros((last - rows, width), jnp.bfloat16)], 0
            )
        else:
            piece = jnp.concatenate([body[first:rows, cols], after[: last - rows, cols]], 0)
        rhs[g, :LANES, at] = piece
        rhs[g, LANES:, at] = piece
    vals[: rows - HALO, cols] = body[rows + HALO :, cols]
    if after is None:
        vals[rows - HALO : rows, cols] = jnp.zeros((HALO, width), jnp.bfloat16)
    else:
        vals[rows - HALO : rows, cols] = after[rows : rows + HALO, cols]


def fold_keys(kp, taps, rhs, h, g, dims):
    rows, _, _, width, q_taps, _ = dims
    for first in range(0, q_taps, FOLD_TAPS):
        last = min(q_taps, first + FOLD_TAPS)
        out = dot(taps[h, first * BLOCK : last * BLOCK], rhs[g])
        for a in range(first, last):
            for blk in range(rows // BLOCK):
                at, row = blk * BLOCK, (a - first) * BLOCK
                high, low = split(out[row : row + BLOCK, blk * width : (blk + 1) * width])
                kp[at : at + BLOCK, a * width : (a + 1) * width] = high
                kp[rows + at : rows + at + BLOCK, a * width : (a + 1) * width] = low


def first_window(kv_ref, g, width):
    cols = slice(g * width, (g + 1) * width)
    zeros = jnp.zeros((HALO, width), jnp.bfloat16)
    rest = jnp.zeros((LANES - 3 * HALO, width), jnp.bfloat16)
    window = jnp.concatenate([zeros, kv_ref[: 2 * HALO, cols], rest], 0)
    return jnp.concatenate([window, window], 0)


def first_folded(taps_ref, window, h, q_taps):
    taps = jnp.concatenate(
        [taps_ref[h, a * BLOCK : a * BLOCK + HALO] for a in range(q_taps)], 0
    )
    folded = dot(taps, window)
    folded = jnp.concatenate([folded[a * HALO : (a + 1) * HALO] for a in range(q_taps)], 1)
    return jnp.concatenate(split(folded), 0)


def update(scores, values, at, h, m_in, l_in, acc_in, m_ref, l_ref, acc_ref):
    old = m_in[h : h + 1, :]
    top = jnp.maximum(old, jnp.max(scores, axis=0, keepdims=True))
    weights = jnp.exp(scores - top)
    decay = jnp.exp(old - top)
    m_ref[h : h + 1, :] = top
    l_ref[h : h + 1, :] = l_in[h : h + 1, :] * decay + jnp.sum(weights, axis=0, keepdims=True)
    acc_ref[h] = acc_in[h] * decay + dot_tn(values[:, at], weights.astype(jnp.bfloat16))


def pack_kernel(dims, q_hbm, k_hbm, v_hbm, e_ref, kv_ref, sems):
    rows, heads, _, width, _, _ = dims
    qcols = heads * width
    moves = (
        (q_hbm.at[rows - HALO :], e_ref.at[:, :qcols]),
        (k_hbm.at[rows - HALO :], e_ref.at[:, qcols:]),
        (k_hbm, kv_ref.at[:rows]),
        (v_hbm, kv_ref.at[rows:]),
    )
    copies = [pltpu.make_async_copy(*move, sems.at[i]) for i, move in enumerate(moves)]
    for copy in copies:
        copy.start()
    for copy in copies:
        copy.wait()


def taps_kernel(dims, conv_hbm, taps_ref, coef_ref, conv, sem):
    _, heads, _, width, q_taps, k_taps = dims
    k_edge = k_taps // 2
    copy = pltpu.make_async_copy(conv_hbm, conv, sem)
    copy.start()
    copy.wait()
    lane = lax.broadcasted_iota(jnp.int32, (heads, LANES), 1)
    owner = lane // (2 * SLOT) + 4 * ((lane // SLOT) % 2)
    spread = jnp.where(
        owner == lax.broadcasted_iota(jnp.int32, (heads, LANES), 0), 1.0, 0.0
    ).astype(jnp.float32)
    offset = lax.broadcasted_iota(jnp.int32, (k_taps, LANES), 1) % SLOT
    tap = lax.broadcasted_iota(jnp.int32, (k_taps, LANES), 0)
    for a in range(q_taps):
        weights = conv[a] * width ** (-0.5)
        base = jnp.zeros((heads, LANES), jnp.float32)
        for t in range(k_taps):
            base = jnp.where(lane == HALO + k_edge - t, weights[:, t : t + 1], base)
        for h in range(heads):
            tile = pltpu.roll(
                jnp.broadcast_to(base[h : h + 1], (BLOCK, LANES)), 0, 1, stride=1, stride_axis=0
            )
            high, low = split(tile)
            taps_ref[h, a * BLOCK : (a + 1) * BLOCK, :LANES] = high
            taps_ref[h, a * BLOCK : (a + 1) * BLOCK, LANES:] = low
        lanes = dot_tn(weights, spread, lax.Precision.HIGHEST)
        source = offset + tap - k_edge - a
        inside = (source >= 0) & (source < SLOT) & (offset < q_taps - 1 + k_edge)
        coef_ref[a * 16 : a * 16 + k_taps] = jnp.where(inside, lanes, 0.0)


def own_kernel(
    dims,
    q_hbm, kv_ref, e_ref, taps_ref, coef,
    qcat_ref, m_ref, l_ref, acc_ref, corner_ref,
    q_ref, qf, rhs, kp0, kp1, sc, vals, rolled, zband, packed_ref, sem,
):
    rows, heads, kv, width, q_taps, k_taps = dims
    per = heads // kv
    k_edge = k_taps // 2
    reach = q_taps - 1 + k_edge
    qcols = heads * width
    copy = pltpu.make_async_copy(q_hbm, q_ref, sem)
    copy.start()
    for g in range(kv):
        fill_group(rhs, vals, g, kv_ref, None, dims)
    copy.wait()
    blocks = rows // LANES
    tall = rows + HALO
    lane = lax.broadcasted_iota(jnp.int32, (tall, LANES), 1)
    sub = lax.broadcasted_iota(jnp.int32, (tall, LANES), 0)
    lane_small = lax.broadcasted_iota(jnp.int32, (HALO, LANES), 1)
    packs = [jnp.zeros((tall, LANES), jnp.float32) for _ in range(2)]
    for h in range(heads):
        g = h // per
        cols = slice(h * width, (h + 1) * width)
        kcols = slice(g * width, (g + 1) * width)
        qf[:HALO] = e_ref[:, cols].astype(jnp.float32)
        qf[HALO:] = q_ref[:, cols].astype(jnp.float32)
        qcat_ref[h, :, :width] = q_ref[:, cols]
        for a in range(1, q_taps):
            qcat_ref[h, :, a * width : (a + 1) * width] = qf[
                HALO - a : HALO - a + rows
            ].astype(jnp.bfloat16)
        near = jnp.concatenate([q_ref[: LANES - HALO, cols], e_ref[:, cols]], 0)
        pieces = [dot_nt(e_ref[:, qcols + g * width : qcols + (g + 1) * width], near)]
        for blk in range(blocks):
            key_blk = kv_ref[blk * LANES : (blk + 1) * LANES, kcols]
            last = min(rows, (blk + 2) * LANES)
            raw = dot_nt(key_blk, q_ref[blk * LANES : last, cols])
            if last == (blk + 2) * LANES:
                pieces.append(raw[: LANES - HALO, :LANES])
                pieces.append(
                    jnp.where(
                        lane_small < LANES // 2,
                        raw[LANES - HALO :, LANES:],
                        raw[LANES - HALO :, :LANES],
                    )
                )
            else:
                pieces.append(raw)
        ring = jnp.concatenate(pieces, 0)
        moved = []
        for first in range(0, tall, 8):
            shift = (slot_lane(h) + HALO - first) % LANES
            part = ring[first : first + 8]
            moved.append(pltpu.roll(part, shift, 1) if shift else part)
        mine = (lane - slot_lane(h)) % LANES < 2 * SLOT
        packs[h // 4] = jnp.where(mine, jnp.concatenate(moved, 0), packs[h // 4])
    for i in range(2 if heads > 4 else 1):
        for bit in (1, 2, 4):
            packs[i] = jnp.where(
                (sub & bit) != 0, pltpu.roll(packs[i], LANES - bit, 1), packs[i]
            )
    packed_ref[...] = jnp.where((lane // SLOT) % 2 == 0, packs[0], packs[1])
    deltas = list(enumerate(range(-k_edge - q_taps + 1, k_edge + 1)))

    def roll_unit(order, delta):
        rolled[order, :8] = jnp.zeros((8, LANES), jnp.float32)
        shift = (-delta) % LANES
        value = packed_ref[...]
        rolled[order, 8 : 8 + tall] = pltpu.roll(value, shift, 1) if shift else value
        rolled[order, 8 + tall :] = jnp.zeros((8, LANES), jnp.float32)

    def band_unit(first):
        total = jnp.zeros((HALO, LANES), jnp.float32)
        for order, delta in deltas:
            for a in range(q_taps):
                t = k_edge + a + delta
                if 0 <= t < k_taps:
                    at = 8 + first + k_edge - t
                    row = a * 16 + t
                    total = total + coef[row : row + 1, :] * rolled[order, at : at + HALO]
        zband[first : first + HALO] = total

    units = [functools.partial(roll_unit, *pair) for pair in deltas]
    units += [functools.partial(band_unit, first) for first in range(0, tall, HALO)]
    zband[tall:] = jnp.zeros((HALO, LANES), jnp.float32)
    key_id = HALO + lax.broadcasted_iota(jnp.int32, (rows, rows), 0)
    row_id = lax.broadcasted_iota(jnp.int32, (rows, rows), 1)

    def finish_head(h):
        g = h // per
        base = slot_lane(h)
        corner_ref[h] = pltpu.roll(
            zband[: 2 * HALO], (LANES - HALO - base) % LANES, 1, stride=1, stride_axis=0
        )
        strips = []
        for blk in range(blocks):
            at = 2 * HALO + blk * LANES
            tile = pltpu.roll(
                zband[at : at + LANES], (HALO - base) % LANES, 1, stride=1, stride_axis=0
            )
            strips.append(jnp.concatenate([tile] * blocks, 1))
        exact = jnp.concatenate(strips, 0)
        scores = jnp.where(row_id - key_id < reach, exact, sc[h])
        scores = jnp.where(key_id <= row_id, scores, NEG_FILL)
        top = jnp.max(scores, axis=0, keepdims=True)
        weights = jnp.where(key_id <= row_id, jnp.exp(scores - top), 0.0)
        m_ref[h : h + 1, :] = top
        l_ref[h : h + 1, :] = jnp.sum(weights, axis=0, keepdims=True)
        acc_ref[h] = dot_tn(vals[:, g * width : (g + 1) * width], weights.astype(jnp.bfloat16))

    kps = (kp0, kp1)
    early = max(1, heads - 3)
    share = -(-len(units) // early)
    done = 0
    for h in range(heads):
        fold_keys(kps[h % 2], taps_ref, rhs, h, h // per, dims)
        if h < early:
            for unit in units[h * share : (h + 1) * share]:
                unit()
        else:
            for _ in range(2):
                if done < h:
                    finish_head(done)
                    done += 1
        both = dot_nt(kps[h % 2][...], qcat_ref[h])
        sc[h] = both[:rows] + both[rows:]
    for h in range(done, heads):
        finish_head(h)


def first_positions(dims, qcat_ref, taps_ref, kv_ref, corner_ref, state_in, state):
    rows, heads, kv, width, q_taps, k_taps = dims
    per = heads // kv
    reach = q_taps - 1 + k_taps // 2
    key_id = lax.broadcasted_iota(jnp.int32, (HALO, rows), 0)
    row_id = lax.broadcasted_iota(jnp.int32, (HALO, rows), 1)
    for h in range(heads):
        g = h // per
        both = dot_nt(first_folded(taps_ref, first_window(kv_ref, g, width), h, q_taps), qcat_ref[h])
        scores = both[:HALO] + both[HALO:]
        exact = jnp.concatenate([corner_ref[h, HALO:]] * (rows // LANES), 1)
        scores = jnp.where(row_id - key_id < reach, exact, scores)
        scores = jnp.where(key_id <= row_id, scores, NEG_FILL)
        at = slice(g * width, (g + 1) * width)
        update(scores, kv_ref.at[rows : rows + HALO], at, h, *state_in, *state)


def add_shard(
    dims, step, extra, qcat_ref, taps_ref, corner_ref, body, after, state_in, state, scratch, finish
):
    rows, heads, kv, width, q_taps, k_taps = dims
    per = heads // kv
    reach = q_taps - 1 + k_taps // 2
    rhs, kp0, kp1, sc0, sc1, vals = scratch
    kps, scs = (kp0, kp1), (sc0, sc1)
    total = rows + HALO if extra else rows
    for g in range(kv):
        fill_group(rhs, vals, g, body, after, dims)
    if extra:
        vals[rows:] = body[rows : rows + HALO]
    key_id = lax.broadcasted_iota(jnp.int32, (2 * HALO, LANES), 0) - HALO
    row_id = lax.broadcasted_iota(jnp.int32, (2 * HALO, LANES), 1)

    def fold(h):
        fold_keys(kps[h % 2], taps_ref, rhs, h, h // per, dims)
        if extra:
            window = first_window(body, h // per, width)
            kps[h % 2][2 * rows :] = first_folded(taps_ref, window, h, q_taps)

    fold(0)
    for h in range(heads):
        g = h // per
        sc = scs[h % 2]
        both = dot_nt(kps[h % 2][: 2 * total], qcat_ref[h])
        sc[:rows] = both[:rows] + both[rows : 2 * rows]
        if extra:
            sc[rows:] = both[2 * rows : 2 * rows + HALO] + both[2 * rows + HALO :]
        if h + 1 < heads:
            fold(h + 1)
        if step == 1:
            at = slice(rows - 2 * HALO, rows)
            patch = sc[at, :LANES]
            patch = jnp.where(row_id - key_id < reach, corner_ref[h], patch)
            sc[at, :LANES] = jnp.where(key_id <= row_id, patch, NEG_FILL)
        at = slice(g * width, (g + 1) * width)
        update(sc[:total], vals.at[:total], at, h, *state_in, *state)
        if finish is not None and h % per == per - 1:
            finish(g)


def step_kernel(
    dims, step, qcat_ref, taps_ref, corner_ref, m_in, l_in, acc_in, after, body,
    m_ref, l_ref, acc_ref, *scratch
):
    place = lax.axis_index("ctx")
    states = (m_in, l_in, acc_in), (m_ref, l_ref, acc_ref)
    fixed = (qcat_ref, taps_ref, corner_ref, body, after, *states, scratch, None)

    @pl.when(place == step)
    def _():
        add_shard(dims, step, True, *fixed)

    @pl.when(place > step)
    def _():
        add_shard(dims, step, False, *fixed)


def last_kernel(
    dims, step, qcat_ref, taps_ref, corner_ref, m_in, l_in, acc_in, after, body, own,
    gain_ref, mix_ref, bounds_ref, o_hbm, m_ref, l_ref, acc_ref, out, sems, *scratch
):
    rows, heads, kv, width, _, _ = dims
    per = heads // kv
    place = lax.axis_index("ctx")
    row_pos = place * rows + lax.broadcasted_iota(jnp.int32, (rows, 1), 0)
    live = (row_pos >= bounds_ref[0]) & (row_pos < bounds_ref[1])
    states = (m_in, l_in, acc_in), (m_ref, l_ref, acc_ref)

    def copy_out(g):
        cols = pl.ds(g * per * width, per * width)
        return pltpu.make_async_copy(out.at[:, cols], o_hbm.at[:, cols], sems.at[g])

    def finish(g):
        probs = [acc_ref[h] * (1.0 / l_ref[h : h + 1, :]) for h in range(g * per, (g + 1) * per)]
        for a in range(per):
            blended = mix_ref[g, a, 0] * probs[0]
            for b in range(1, per):
                blended = blended + mix_ref[g, a, b] * probs[b]
            mean_sq = jnp.mean(blended * blended, axis=0, keepdims=True)
            normed = (blended * lax.rsqrt(mean_sq + EPSILON)).T
            at = slice((g * per + a) * width, (g * per + a + 1) * width)
            normed = jnp.where(live, normed * gain_ref[:, at], 0.0)
            out[:, at] = normed.astype(jnp.bfloat16)
        copy_out(g).start()

    @pl.when(place == step)
    def _():
        add_shard(
            dims, step, True, qcat_ref, taps_ref, corner_ref, body, after, *states, scratch, finish
        )

    @pl.when(place < step)
    def _():
        @pl.when(place == 0)
        def _():
            first_positions(dims, qcat_ref, taps_ref, own, corner_ref, *states)

        @pl.when(place > 0)
        def _():
            l_ref[...] = l_in[...]
            acc_ref[...] = acc_in[...]

        for g in range(kv):
            finish(g)

    for g in range(kv):
        copy_out(g).wait()


VMEM = pl.BlockSpec(memory_space=pltpu.VMEM)
SMEM = pl.BlockSpec(memory_space=pltpu.SMEM)
HBM = pl.BlockSpec(memory_space=pltpu.HBM)


def send(value, pairs):
    return lax.ppermute(value, "ctx", pairs)


def cost(flops):
    return pl.CostEstimate(flops=flops, bytes_accessed=2**20, transcendentals=0)


def attend(queries, keys, values, conv_kernel, head_mix, norm_gain, bounds):
    rows = queries.shape[0]
    kv, _ = head_mix.shape[:2]
    width = keys.shape[1] // kv
    heads, q_taps, k_taps = conv_kernel.shape
    count = lax.axis_size("ctx")
    dims = (rows, heads, kv, width, q_taps, k_taps)
    f32, bf16 = jnp.float32, jnp.bfloat16
    params = pltpu.CompilerParams(vmem_limit_bytes=28 * 2**20)

    columns = kv * width
    taps_in = conv_kernel.transpose(1, 0, 2)
    queries, keys, values, taps_in = (
        pltpu.with_memory_space_constraint(value, pltpu.HBM)
        for value in (queries, keys, values, taps_in)
    )
    edges, own = pl.pallas_call(
        functools.partial(pack_kernel, dims),
        name="pack",
        out_shape=(
            pltpu.VMEM((HALO, heads * width + columns), bf16),
            pltpu.VMEM((2 * rows, columns), bf16),
        ),
        in_specs=[HBM, HBM, HBM],
        out_specs=(VMEM,) * 2,
        scratch_shapes=[pltpu.SemaphoreType.DMA((4,))],
        compiler_params=params,
    )(queries, keys, values)
    edges = send(edges, [(at, at + 1) for at in range(count - 1)])
    first = send(own, [(at, at + 1) for at in range(count - 1)])

    def scratch(extra):
        return [
            pltpu.VMEM((kv, 2 * LANES, rows // BLOCK * width), bf16),
            pltpu.VMEM((2 * (rows + extra), q_taps * width), bf16),
            pltpu.VMEM((2 * (rows + extra), q_taps * width), bf16),
            pltpu.VMEM((rows + extra, rows), f32),
            pltpu.VMEM((rows + extra, rows), f32),
            pltpu.VMEM((rows + extra, columns), bf16),
        ]

    state = [
        pltpu.VMEM((heads, rows), f32),
        pltpu.VMEM((heads, rows), f32),
        pltpu.VMEM((heads, width, rows), f32),
    ]
    taps, coef = pl.pallas_call(
        functools.partial(taps_kernel, dims),
        name="taps",
        out_shape=(
            pltpu.VMEM((heads, q_taps * BLOCK, 2 * LANES), bf16),
            pltpu.VMEM((q_taps * 16, LANES), f32),
        ),
        in_specs=[HBM],
        out_specs=(VMEM, VMEM),
        scratch_shapes=[pltpu.VMEM((q_taps, heads, k_taps), f32), pltpu.SemaphoreType.DMA],
        compiler_params=params,
        cost_estimate=cost(10**9),
    )(taps_in)
    edges, taps = lax.optimization_barrier((edges, taps))
    qcat, top, total, acc, corner = pl.pallas_call(
        functools.partial(own_kernel, dims),
        name="own_shard",
        out_shape=(
            pltpu.VMEM((heads, rows, q_taps * width), bf16),
            *state,
            pltpu.VMEM((heads, 2 * HALO, LANES), f32),
        ),
        in_specs=[HBM] + [VMEM] * 4,
        out_specs=(VMEM,) * 5,
        scratch_shapes=[
            pltpu.VMEM((rows, heads * width), bf16),
            pltpu.VMEM((rows + HALO, width), f32),
            *scratch(0)[:3],
            pltpu.VMEM((heads, rows, rows), f32),
            pltpu.VMEM((rows, columns), bf16),
            pltpu.VMEM((q_taps + k_taps - 1, rows + HALO + 16, LANES), f32),
            pltpu.VMEM((rows + 2 * HALO, LANES), f32),
            pltpu.VMEM((rows + HALO, LANES), f32),
            pltpu.SemaphoreType.DMA,
        ],
        compiler_params=params,
        cost_estimate=cost(6 * 10**9),
    )(queries, own, edges, taps, coef)
    before, message = own, first
    for step in range(1, count - 1):
        source, top = lax.optimization_barrier((message, top))
        passed = send(source, [(at, at + 1) for at in range(step, count - 1)])
        top, total, acc = pl.pallas_call(
            functools.partial(step_kernel, dims, step),
            name="shard_step",
            out_shape=tuple(state),
            in_specs=[VMEM] * 8,
            out_specs=(VMEM,) * 3,
            scratch_shapes=scratch(HALO),
            input_output_aliases={3: 0, 4: 1, 5: 2},
            compiler_params=params,
            cost_estimate=cost(5 * 10**9),
        )(qcat, taps, corner, top, total, acc, before, message)
        before, message = message, passed
    return pl.pallas_call(
        functools.partial(last_kernel, dims, count - 1),
        name="last_step",
        out_shape=jax.ShapeDtypeStruct((rows, heads * width), bf16),
        in_specs=[VMEM] * 10 + [SMEM] * 2,
        out_specs=HBM,
        scratch_shapes=[
            *state,
            pltpu.VMEM((rows, heads * width), bf16),
            pltpu.SemaphoreType.DMA((kv,)),
            *scratch(HALO),
        ],
        compiler_params=params,
        cost_estimate=cost(5 * 10**9),
    )(
        qcat, taps, corner, top, total, acc, before, message, own,
        norm_gain.reshape(1, -1), head_mix, bounds,
    )


def solution(mesh):
    return jax.shard_map(
        attend,
        mesh=mesh,
        in_specs=(
            P(("groups", "ctx"), "heads"),
            P(("groups", "ctx"), "heads"),
            P(("groups", "ctx"), "heads"),
            P("heads", None, None),
            P("heads", None, None),
            P("heads"),
            P("groups"),
        ),
        out_specs=P(("groups", "ctx"), "heads"),
        check_vma=False,
    )
```

time: 41.8 us -> 39.5 us (0.945)
  the two profiles are of different devices: /device:TPU:20 before, /device:TPU:24 now
where the time goes in v2:
time: 39.5 us; the launch traced here: 39.2 us
  Pallas kernels  26.8 us (68%)
  waiting for transfers between devices  6.94 us (18%)
  starting transfers between devices  5.16 us (13%)
    pallas_call x2, Pallas kernels, attend(): pl.pallas_call(functools.partial(step_kernel, dims, step), name='shard_st...  10.5 us
    pallas_call x1, Pallas kernels, attend(): pl.pallas_call(functools.partial(last_kernel, dims, count - 1), name='las...  7.05 us
    ppermute x4, waiting for transfers between devices, send(): return lax.ppermute(value, 'ctx', pairs)  6.94 us
    pallas_call x1, Pallas kernels, attend(): pl.pallas_call(functools.partial(own_kernel, dims), name='own_shard', out...  6.4 us
    ppermute x4, starting transfers between devices, send(): return lax.ppermute(value, 'ctx', pairs)  5.16 us
    pallas_call x1, Pallas kernels, attend(): pl.pallas_call(functools.partial(taps_kernel, dims), name='taps', out_sha...  1.8 us
    pallas_call x1, Pallas kernels, attend(): pl.pallas_call(functools.partial(pack_kernel, dims), name='pack', out_sha...  1.04 us
  transfers between devices with their start and end apart: 4, of which 3 were waited for; matrix products, arithmetic and copies ran while one was open for 0% of the time, Pallas kernels for 48%

profile of v2, /device:TPU:24, one launch (start us, length us, event | category | flops | bytes accessed | tf_op | source)
XLA Modules:
  0.0 39.2 jit_solution(14769471288102625184)
XLA Ops:
  0.0 1.0 %pack.1 = (bf16[16,1280]{1,0:T(8,128)(2,1)S(1)}, bf16[512,256]{1,0:T(8,128)(2,1)S(1)}) custom-call(bf16[256,1024]{1,0:T(8,128)(2,1)} %q_hbm.3, bf16[256,256]{1,0:T(8,128)(2,1)} %k_hbm.1, bf16[256,256]{1,0:T(8,128)(2,1)} %v_hbm.1), custom_call_target="tpu_custom_call" | custom-call | tf_op jit(solution)/shard_map/pack/pallas_call | solution.py:442
  1.0 1.3 %collective-permute-start = (bf16[16,1280]{1,0:T(8,128)(2,1)S(1)}, bf16[16,1280]{1,0:T(8,128)(2,1)S(1)}, u32[]{:S(2)}, u32[]{:S(2)}) collective-permute-start(bf16[16,1280]{1,0:T(8,128)(2,1)S(1)} %get-tuple-element.27), channel_id=1, source_target_pairs={{0,4},{4,8},{8,12},{1,5},{5,9},{9,13},{2,6},{6,10},{10,14},{3,7},{... | collective-permute-start | bytes 122888 | tf_op jit(solution)/shard_map/ppermute | solution.py:419
  2.3 1.3 %collective-permute-start.1 = (bf16[512,256]{1,0:T(8,128)(2,1)S(1)}, bf16[512,256]{1,0:T(8,128)(2,1)S(1)}, u32[]{:S(2)}, u32[]{:S(2)}) collective-permute-start(bf16[512,256]{1,0:T(8,128)(2,1)S(1)} %get-tuple-element.26.kv_ref.after.own), channel_id=1, source_target_pairs={{0,4},{4,8},{8,12},{1,5},{5,9},{9,13},{2,6},{6,10},{10,14},{3,7},{... | collective-permute-start | bytes 786440 | tf_op jit(solution)/shard_map/ppermute | solution.py:419
  3.6 1.8 %taps.1 = (bf16[8,384,256]{2,1,0:T(8,128)(2,1)S(1)}, f32[96,128]{1,0:T(8,128)S(1)}) custom-call(f32[6,8,11]{2,1,0:T(8,128)} %bitcast.3), custom_call_target="tpu_custom_call" | custom-call | flops 1000000000 | bytes 1048576 | tf_op jit(solution)/shard_map/taps/pallas_call | solution.py:472
  5.4 1.5 %collective-permute-done.e_ref = bf16[16,1280]{1,0:T(8,128)(2,1)S(1)} collective-permute-done((bf16[16,1280]{1,0:T(8,128)(2,1)S(1)}, bf16[16,1280]{1,0:T(8,128)(2,1)S(1)}, u32[]{:S(2)}, u32[]{:S(2)}) %collective-permute-start) | collective-permute-done | bytes 40992 | tf_op jit(solution)/shard_map/ppermute | solution.py:419
  6.9 6.4 %own_shard.1 = (bf16[8,256,768]{2,1,0:T(8,128)(2,1)S(1)}, f32[8,256]{1,0:T(8,128)S(1)}, f32[8,256]{1,0:T(8,128)S(1)}, f32[8,128,256]{2,1,0:T(8,128)S(1)}, f32[8,32,128]{2,1,0:T(8,128)S(1)}) custom-call(bf16[256,1024]{1,0:T(8,128)(2,1)} %q_hbm.3, bf16[512,256]{1,0:T(8,128)(2,1)S(1)} %get-tuple-element.26.kv_ref.after.own, ...), custom_call_target="tpu_custom_call" | custom-call | flops 6000000000 | bytes 1048576 | tf_op jit(solution)/shard_map/own_shard/pallas_call | solution.py:486
  13.3 0.0 collective-permute-done.1.body.after
  13.4 1.3 %collective-permute-start.2 = (bf16[512,256]{1,0:T(8,128)(2,1)S(1)}, bf16[512,256]{1,0:T(8,128)(2,1)S(1)}, u32[]{:S(2)}, u32[]{:S(2)}) collective-permute-start(bf16[512,256]{1,0:T(8,128)(2,1)S(1)} %collective-permute-done.1.body.after), channel_id=1, source_target_pairs={{4,8},{8,12},{5,9},{9,13},{6,10},{10,14},{7,11},{11,15},{20,24},{2... | collective-permute-start | bytes 786440 | tf_op jit(solution)/shard_map/ppermute | solution.py:419
  14.7 5.2 %shard_step.2 = (f32[8,256]{1,0:T(8,128)S(1)}, f32[8,256]{1,0:T(8,128)S(1)}, f32[8,128,256]{2,1,0:T(8,128)S(1)}) custom-call(bf16[8,256,768]{2,1,0:T(8,128)(2,1)S(1)} %get-tuple-element.32.qcat_ref, bf16[8,384,256]{2,1,0:T(8,128)(2,1)S(1)} %get-tuple-element.30.taps_ref, ...), custom_call_target="tpu_custom_call", output_to_operand_aliasing={{0}: (3, {}), {1}: (4, {}), {2}: (5, {})} | custom-call | flops 5000000000 | bytes 1048576 | tf_op jit(solution)/shard_map/shard_step/pallas_call | solution.py:514
  19.9 3.2 %collective-permute-done.2.body.after = bf16[512,256]{1,0:T(8,128)(2,1)S(1)} collective-permute-done((bf16[512,256]{1,0:T(8,128)(2,1)S(1)}, bf16[512,256]{1,0:T(8,128)(2,1)S(1)}, u32[]{:S(2)}, u32[]{:S(2)}) %collective-permute-start.2) | collective-permute-done | bytes 262176 | tf_op jit(solution)/shard_map/ppermute | solution.py:419
  23.1 1.3 %collective-permute-start.3 = (bf16[512,256]{1,0:T(8,128)(2,1)S(1)}, bf16[512,256]{1,0:T(8,128)(2,1)S(1)}, u32[]{:S(2)}, u32[]{:S(2)}) collective-permute-start(bf16[512,256]{1,0:T(8,128)(2,1)S(1)} %collective-permute-done.2.body.after), channel_id=1, source_target_pairs={{8,12},{9,13},{10,14},{11,15},{24,28},{25,29},{26,30},{27,31}} | collective-permute-start | bytes 786440 | tf_op jit(solution)/shard_map/ppermute | solution.py:419
  24.4 0.0 copy-start
  24.4 0.0 copy-start.1
  24.4 0.0 copy-start.2
  24.4 5.3 %shard_step.3 = (f32[8,256]{1,0:T(8,128)S(1)}, f32[8,256]{1,0:T(8,128)S(1)}, f32[8,128,256]{2,1,0:T(8,128)S(1)}) custom-call(bf16[8,256,768]{2,1,0:T(8,128)(2,1)S(1)} %get-tuple-element.32.qcat_ref, bf16[8,384,256]{2,1,0:T(8,128)(2,1)S(1)} %get-tuple-element.30.taps_ref, ...), custom_call_target="tpu_custom_call", output_to_operand_aliasing={{0}: (3, {}), {1}: (4, {}), {2}: (5, {})} | custom-call | flops 5000000000 | bytes 1048576 | tf_op jit(solution)/shard_map/shard_step/pallas_call | solution.py:514
  29.7 2.3 %collective-permute-done.3.body = bf16[512,256]{1,0:T(8,128)(2,1)S(1)} collective-permute-done((bf16[512,256]{1,0:T(8,128)(2,1)S(1)}, bf16[512,256]{1,0:T(8,128)(2,1)S(1)}, u32[]{:S(2)}, u32[]{:S(2)}) %collective-permute-start.3) | collective-permute-done | bytes 262176 | tf_op jit(solution)/shard_map/ppermute | solution.py:419
  31.9 0.0 copy-done
  31.9 0.0 copy-done.1
  31.9 0.0 copy-done.2
  31.9 7.1 %last_step.1 = bf16[256,1024]{1,0:T(8,128)(2,1)} custom-call(bf16[8,256,768]{2,1,0:T(8,128)(2,1)S(1)} %get-tuple-element.32.qcat_ref, bf16[8,384,256]{2,1,0:T(8,128)(2,1)S(1)} %get-tuple-element.30.taps_ref, f32[8,32,128]{2,1,0:T(8,128)S(1)} %get-tuple-element.33.corner_ref, f32[8,256]{1,0:T(8,128)S(1)} %get-tuple-element.43.m_in, ...), custom_call_target="tpu_custom_call" | custom-call | flops 5000000000 | bytes 1048576 | tf_op jit(solution)/shard_map/last_step/pallas_call | solution.py:526
Async XLA Ops:
  1.0 5.9 %collective-permute-start = (bf16[16,1280]{1,0:T(8,128)(2,1)S(1)}, bf16[16,1280]{1,0:T(8,128)(2,1)S(1)}, u32[]{:S(2)}, u32[]{:S(2)}) collective-permute-start(bf16[16,1280]{1,0:T(8,128)(2,1)S(1)} %get-tuple-element.27), channel_id=1, source_target_pairs={{0,4},{4,8},{8,12},{1,5},{5,9},{9,13},{2,6},{6,10},{10,14},{3,7},{... | collective-permute-start | bytes 122888 | tf_op jit(solution)/shard_map/ppermute | solution.py:419
  2.3 11.0 %collective-permute-start.1 = (bf16[512,256]{1,0:T(8,128)(2,1)S(1)}, bf16[512,256]{1,0:T(8,128)(2,1)S(1)}, u32[]{:S(2)}, u32[]{:S(2)}) collective-permute-start(bf16[512,256]{1,0:T(8,128)(2,1)S(1)} %get-tuple-element.26.kv_ref.after.own), channel_id=1, source_target_pairs={{0,4},{4,8},{8,12},{1,5},{5,9},{9,13},{2,6},{6,10},{10,14},{3,7},{... | collective-permute-start | bytes 786440 | tf_op jit(solution)/shard_map/ppermute | solution.py:419
  13.4 9.7 %collective-permute-start.2 = (bf16[512,256]{1,0:T(8,128)(2,1)S(1)}, bf16[512,256]{1,0:T(8,128)(2,1)S(1)}, u32[]{:S(2)}, u32[]{:S(2)}) collective-permute-start(bf16[512,256]{1,0:T(8,128)(2,1)S(1)} %collective-permute-done.1.body.after), channel_id=1, source_target_pairs={{4,8},{8,12},{5,9},{9,13},{6,10},{10,14},{7,11},{11,15},{20,24},{2... | collective-permute-start | bytes 786440 | tf_op jit(solution)/shard_map/ppermute | solution.py:419
  23.1 8.8 %collective-permute-start.3 = (bf16[512,256]{1,0:T(8,128)(2,1)S(1)}, bf16[512,256]{1,0:T(8,128)(2,1)S(1)}, u32[]{:S(2)}, u32[]{:S(2)}) collective-permute-start(bf16[512,256]{1,0:T(8,128)(2,1)S(1)} %collective-permute-done.2.body.after), channel_id=1, source_target_pairs={{8,12},{9,13},{10,14},{11,15},{24,28},{25,29},{26,30},{27,31}} | collective-permute-start | bytes 786440 | tf_op jit(solution)/shard_map/ppermute | solution.py:419
  24.4 7.6 %copy-start = (f32[1024]{0:T(1024)S(1)}, f32[1024]{0:T(1024)}, u32[]{:S(2)}) copy-start(f32[1024]{0:T(1024)} %param.12) | copy-start | bytes 12292
  24.4 7.6 %copy-start.1 = (f32[2,4,4]{2,1,0:T(4,128)S(1)}, f32[2,4,4]{2,1,0:T(4,128)}, u32[]{:S(2)}) copy-start(f32[2,4,4]{2,1,0:T(4,128)} %mix_ref.1) | copy-start | bytes 388
  24.4 7.5 %copy-start.2 = (s32[2]{0:T(128)S(1)}, s32[2]{0:T(128)}, u32[]{:S(2)}) copy-start(s32[2]{0:T(128)} %bounds_ref.1) | copy-start | bytes 28

commit v3 on v2

--- a/solution.py
+++ b/solution.py
@@ -13,6 +13,7 @@
 HALO = 16
 BLOCK = 64
 SLOT = 16
+TAIL = 8
 FOLD_TAPS = 2
 
 
@@ -55,7 +56,7 @@
             piece = jnp.concatenate([body[first:rows, cols], after[: last - rows, cols]], 0)
         rhs[g, :LANES, at] = piece
         rhs[g, LANES:, at] = piece
-    vals[: rows - HALO, cols] = body[rows + HALO :, cols]
+    vals[: rows - HALO, cols] = body[rows + HALO : 2 * rows, cols]
     if after is None:
         vals[rows - HALO : rows, cols] = jnp.zeros((HALO, width), jnp.bfloat16)
     else:
@@ -102,15 +103,14 @@
     acc_ref[h] = acc_in[h] * decay + dot_tn(values[:, at], weights.astype(jnp.bfloat16))
 
 
-def pack_kernel(dims, q_hbm, k_hbm, v_hbm, e_ref, kv_ref, sems):
-    rows, heads, _, width, _, _ = dims
-    qcols = heads * width
-    moves = (
-        (q_hbm.at[rows - HALO :], e_ref.at[:, :qcols]),
-        (k_hbm.at[rows - HALO :], e_ref.at[:, qcols:]),
-        (k_hbm, kv_ref.at[:rows]),
-        (v_hbm, kv_ref.at[rows:]),
-    )
+def pack_kernel(dims, q_hbm, k_hbm, v_hbm, own_ref, sems):
+    rows, _, kv, width, _, _ = dims
+    columns = kv * width
+    moves = [(k_hbm, own_ref.at[:rows]), (v_hbm, own_ref.at[rows : 2 * rows])]
+    for i in range(q_hbm.shape[1] // columns):
+        at = 2 * rows + i * TAIL
+        source = q_hbm.at[rows - TAIL :, i * columns : (i + 1) * columns]
+        moves.append((source, own_ref.at[at : at + TAIL]))
     copies = [pltpu.make_async_copy(*move, sems.at[i]) for i, move in enumerate(moves)]
     for copy in copies:
         copy.start()
@@ -149,17 +149,91 @@
         coef_ref[a * 16 : a * 16 + k_taps] = jnp.where(inside, lanes, 0.0)
 
 
+def pack_head(packs, ring, h):
+    lane = lax.broadcasted_iota(jnp.int32, ring.shape, 1)
+    moved = []
+    for first in range(0, ring.shape[0], 8):
+        shift = (slot_lane(h) + HALO - first) % LANES
+        piece = ring[first : first + 8]
+        moved.append(pltpu.roll(piece, shift, 1) if shift else piece)
+    mine = (lane - slot_lane(h)) % LANES < 2 * SLOT
+    packs[h // 4] = jnp.where(mine, jnp.concatenate(moved, 0), packs[h // 4])
+
+
+def skew(packs, heads):
+    sub = lax.broadcasted_iota(jnp.int32, packs[0].shape, 0)
+    for i in range(2 if heads > 4 else 1):
+        for bit in (1, 2, 4):
+            packs[i] = jnp.where(
+                (sub & bit) != 0, pltpu.roll(packs[i], LANES - bit, 1), packs[i]
+            )
+
+
+def roll_band(rolled, packed_ref, order, delta):
+    tall = packed_ref.shape[0]
+    rolled[order, :8] = jnp.zeros((8, LANES), jnp.float32)
+    shift = (-delta) % LANES
+    value = packed_ref[...]
+    rolled[order, 8 : 8 + tall] = pltpu.roll(value, shift, 1) if shift else value
+    rolled[order, 8 + tall :] = jnp.zeros((8, LANES), jnp.float32)
+
+
+def convolve_band(zband, rolled, coef, deltas, q_taps, k_taps, first):
+    k_edge = k_taps // 2
+    total = jnp.zeros((HALO, LANES), jnp.float32)
+    for order, delta in deltas:
+        for a in range(q_taps):
+            t = k_edge + a + delta
+            if 0 <= t < k_taps:
+                at = 8 + first + k_edge - t
+                row = a * 16 + t
+                total = total + coef[row : row + 1, :] * rolled[order, at : at + HALO]
+    zband[first : first + HALO] = total
+
+
+def edge_kernel(dims, below, own, coef, qcat_in, qcat_ref, corner_ref, rolled, packed_ref, zband):
+    rows, heads, kv, width, q_taps, k_taps = dims
+    per = heads // kv
+    k_edge = k_taps // 2
+    tall = packed_ref.shape[0]
+    lane = lax.broadcasted_iota(jnp.int32, (tall, LANES), 1)
+    packs = [jnp.zeros((tall, LANES), jnp.float32) for _ in range(2)]
+    for h in range(heads):
+        g = h // per
+        cols = slice(g * width, (g + 1) * width)
+        at = 2 * rows + h // kv * TAIL
+        tail = below[at : at + TAIL, h % kv * width : (h % kv + 1) * width].astype(jnp.float32)
+        joined = jnp.concatenate([tail, qcat_in[h, :HALO, :width].astype(jnp.float32)], 0)
+        for a in range(1, q_taps):
+            shifted = joined[TAIL - a : TAIL - a + HALO].astype(jnp.bfloat16)
+            qcat_ref[h, :HALO, a * width : (a + 1) * width] = shifted
+        zeros = jnp.zeros((HALO - TAIL, width), jnp.float32)
+        tail = jnp.concatenate([zeros, tail], 0).astype(jnp.bfloat16)
+        near = jnp.concatenate([qcat_in[h, : LANES - HALO, :width], tail], 0)
+        keys = jnp.concatenate([below[rows - HALO : rows, cols], own[: tall - HALO, cols]], 0)
+        pack_head(packs, dot_nt(keys, near), h)
+    skew(packs, heads)
+    packed_ref[...] = jnp.where((lane // SLOT) % 2 == 0, packs[0], packs[1])
+    deltas = list(enumerate(range(-k_edge - q_taps + 1, k_edge + 1)))
+    for pair in deltas:
+        roll_band(rolled, packed_ref, *pair)
+    for first in (0, HALO):
+        convolve_band(zband, rolled, coef, deltas, q_taps, k_taps, first)
+    for h in range(heads):
+        shift = (LANES - HALO - slot_lane(h)) % LANES
+        corner_ref[h] = pltpu.roll(zband[...], shift, 1, stride=1, stride_axis=0)
+
+
 def own_kernel(
     dims,
-    q_hbm, kv_ref, e_ref, taps_ref, coef,
-    qcat_ref, m_ref, l_ref, acc_ref, corner_ref,
+    q_hbm, kv_ref, taps_ref, coef,
+    qcat_ref, m_ref, l_ref, acc_ref,
     q_ref, qf, rhs, kp0, kp1, sc, vals, rolled, zband, packed_ref, sem,
 ):
     rows, heads, kv, width, q_taps, k_taps = dims
     per = heads // kv
     k_edge = k_taps // 2
     reach = q_taps - 1 + k_edge
-    qcols = heads * width
     copy = pltpu.make_async_copy(q_hbm, q_ref, sem)
     copy.start()
     for g in range(kv):
@@ -168,22 +242,20 @@
     blocks = rows // LANES
     tall = rows + HALO
     lane = lax.broadcasted_iota(jnp.int32, (tall, LANES), 1)
-    sub = lax.broadcasted_iota(jnp.int32, (tall, LANES), 0)
     lane_small = lax.broadcasted_iota(jnp.int32, (HALO, LANES), 1)
     packs = [jnp.zeros((tall, LANES), jnp.float32) for _ in range(2)]
     for h in range(heads):
         g = h // per
         cols = slice(h * width, (h + 1) * width)
         kcols = slice(g * width, (g + 1) * width)
-        qf[:HALO] = e_ref[:, cols].astype(jnp.float32)
+        qf[:HALO] = jnp.zeros((HALO, width), jnp.float32)
         qf[HALO:] = q_ref[:, cols].astype(jnp.float32)
         qcat_ref[h, :, :width] = q_ref[:, cols]
         for a in range(1, q_taps):
             qcat_ref[h, :, a * width : (a + 1) * width] = qf[
                 HALO - a : HALO - a + rows
             ].astype(jnp.bfloat16)
-        near = jnp.concatenate([q_ref[: LANES - HALO, cols], e_ref[:, cols]], 0)
-        pieces = [dot_nt(e_ref[:, qcols + g * width : qcols + (g + 1) * width], near)]
+        pieces = [jnp.zeros((HALO, LANES), jnp.float32)]
         for blk in range(blocks):
             key_blk = kv_ref[blk * LANES : (blk + 1) * LANES, kcols]
             last = min(rows, (blk + 2) * LANES)
@@ -200,39 +272,12 @@
             else:
                 pieces.append(raw)
         ring = jnp.concatenate(pieces, 0)
-        moved = []
-        for first in range(0, tall, 8):
-            shift = (slot_lane(h) + HALO - first) % LANES
-            part = ring[first : first + 8]
-            moved.append(pltpu.roll(part, shift, 1) if shift else part)
-        mine = (lane - slot_lane(h)) % LANES < 2 * SLOT
-        packs[h // 4] = jnp.where(mine, jnp.concatenate(moved, 0), packs[h // 4])
-    for i in range(2 if heads > 4 else 1):
-        for bit in (1, 2, 4):
-            packs[i] = jnp.where(
-                (sub & bit) != 0, pltpu.roll(packs[i], LANES - bit, 1), packs[i]
-            )
+        pack_head(packs, ring, h)
+    skew(packs, heads)
     packed_ref[...] = jnp.where((lane // SLOT) % 2 == 0, packs[0], packs[1])
     deltas = list(enumerate(range(-k_edge - q_taps + 1, k_edge + 1)))
-
-    def roll_unit(order, delta):
-        rolled[order, :8] = jnp.zeros((8, LANES), jnp.float32)
-        shift = (-delta) % LANES
-        value = packed_ref[...]
-        rolled[order, 8 : 8 + tall] = pltpu.roll(value, shift, 1) if shift else value
-        rolled[order, 8 + tall :] = jnp.zeros((8, LANES), jnp.float32)
-
-    def band_unit(first):
-        total = jnp.zeros((HALO, LANES), jnp.float32)
-        for order, delta in deltas:
-            for a in range(q_taps):
-                t = k_edge + a + delta
-                if 0 <= t < k_taps:
-                    at = 8 + first + k_edge - t
-                    row = a * 16 + t
-                    total = total + coef[row : row + 1, :] * rolled[order, at : at + HALO]
-        zband[first : first + HALO] = total
-
+    roll_unit = functools.partial(roll_band, rolled, packed_ref)
+    band_unit = functools.partial(convolve_band, zband, rolled, coef, deltas, q_taps, k_taps)
     units = [functools.partial(roll_unit, *pair) for pair in deltas]
     units += [functools.partial(band_unit, first) for first in range(0, tall, HALO)]
     zband[tall:] = jnp.zeros((HALO, LANES), jnp.float32)
@@ -242,9 +287,6 @@
     def finish_head(h):
         g = h // per
         base = slot_lane(h)
-        corner_ref[h] = pltpu.roll(
-            zband[: 2 * HALO], (LANES - HALO - base) % LANES, 1, stride=1, stride_axis=0
-        )
         strips = []
         for blk in range(blocks):
             at = 2 * HALO + blk * LANES
@@ -439,19 +481,16 @@
         pltpu.with_memory_space_constraint(value, pltpu.HBM)
         for value in (queries, keys, values, taps_in)
     )
-    edges, own = pl.pallas_call(
+    stacked = heads // kv
+    own = pl.pallas_call(
         functools.partial(pack_kernel, dims),
         name="pack",
-        out_shape=(
-            pltpu.VMEM((HALO, heads * width + columns), bf16),
-            pltpu.VMEM((2 * rows, columns), bf16),
-        ),
+        out_shape=pltpu.VMEM((2 * rows + stacked * TAIL, columns), bf16),
         in_specs=[HBM, HBM, HBM],
-        out_specs=(VMEM,) * 2,
-        scratch_shapes=[pltpu.SemaphoreType.DMA((4,))],
+        out_specs=VMEM,
+        scratch_shapes=[pltpu.SemaphoreType.DMA((2 + stacked,))],
         compiler_params=params,
     )(queries, keys, values)
-    edges = send(edges, [(at, at + 1) for at in range(count - 1)])
     first = send(own, [(at, at + 1) for at in range(count - 1)])
 
     def scratch(extra):
@@ -482,17 +521,15 @@
         compiler_params=params,
         cost_estimate=cost(10**9),
     )(taps_in)
-    edges, taps = lax.optimization_barrier((edges, taps))
-    qcat, top, total, acc, corner = pl.pallas_call(
+    qcat, top, total, acc = pl.pallas_call(
         functools.partial(own_kernel, dims),
         name="own_shard",
         out_shape=(
             pltpu.VMEM((heads, rows, q_taps * width), bf16),
             *state,
-            pltpu.VMEM((heads, 2 * HALO, LANES), f32),
         ),
-        in_specs=[HBM] + [VMEM] * 4,
-        out_specs=(VMEM,) * 5,
+        in_specs=[HBM] + [VMEM] * 3,
+        out_specs=(VMEM,) * 4,
         scratch_shapes=[
             pltpu.VMEM((rows, heads * width), bf16),
             pltpu.VMEM((rows + HALO, width), f32),
@@ -506,11 +543,34 @@
         ],
         compiler_params=params,
         cost_estimate=cost(6 * 10**9),
-    )(queries, own, edges, taps, coef)
-    before, message = own, first
-    for step in range(1, count - 1):
-        source, top = lax.optimization_barrier((message, top))
-        passed = send(source, [(at, at + 1) for at in range(step, count - 1)])
+    )(queries, own, taps, coef)
+    before, message, passed = own, first, None
+    corner = None
+    for step in range(1, count):
+        if step + 1 < count:
+            source, top = lax.optimization_barrier((message, top))
+            passed = send(source, [(at, at + 1) for at in range(step, count - 1)])
+        if step == 1:
+            qcat, corner = pl.pallas_call(
+                functools.partial(edge_kernel, dims),
+                name="edge",
+                out_shape=(
+                    pltpu.VMEM((heads, rows, q_taps * width), bf16),
+                    pltpu.VMEM((heads, 2 * HALO, LANES), f32),
+                ),
+                in_specs=[VMEM] * 4,
+                out_specs=(VMEM,) * 2,
+                scratch_shapes=[
+                    pltpu.VMEM((q_taps + k_taps - 1, 3 * HALO + 16, LANES), f32),
+                    pltpu.VMEM((3 * HALO, LANES), f32),
+                    pltpu.VMEM((2 * HALO, LANES), f32),
+                ],
+                input_output_aliases={3: 0},
+                compiler_params=params,
+                cost_estimate=cost(10**9),
+            )(message, own, coef, qcat)
+        if step + 1 == count:
+            break
         top, total, acc = pl.pallas_call(
             functools.partial(step_kernel, dims, step),
             name="shard_step",

time: 39.5 us -> 37.1 us (0.939)
  the two profiles are of different devices: /device:TPU:24 before, /device:TPU:30 now
where the time goes in v3:
time: 37.1 us; the launch traced here: 36.8 us
  Pallas kernels  27.1 us (73%)
  waiting for transfers between devices  5.59 us (15%)
  starting transfers between devices  3.85 us (10%)
    pallas_call x2, Pallas kernels, attend(): pl.pallas_call(functools.partial(step_kernel, dims, step), name='shard_st...  10.5 us
    pallas_call x1, Pallas kernels, attend(): pl.pallas_call(functools.partial(last_kernel, dims, count - 1), name='las...  7.04 us
    pallas_call x1, Pallas kernels, attend(): pl.pallas_call(functools.partial(own_kernel, dims), name='own_shard', out...  5.79 us
    ppermute x3, waiting for transfers between devices, send(): return lax.ppermute(value, 'ctx', pairs)  5.59 us
    ppermute x3, starting transfers between devices, send(): return lax.ppermute(value, 'ctx', pairs)  3.85 us
    pallas_call x1, Pallas kernels, attend(): pl.pallas_call(functools.partial(taps_kernel, dims), name='taps', out_sha...  1.8 us
    pallas_call x1, Pallas kernels, attend(): pl.pallas_call(functools.partial(pack_kernel, dims), name='pack', out_sha...  1.03 us
    pallas_call x1, Pallas kernels, attend(): pl.pallas_call(functools.partial(edge_kernel, dims), name='edge', out_sha...  0.93 us
  transfers between devices with their start and end apart: 3, of which 3 were waited for; matrix products, arithmetic and copies ran while one was open for 0% of the time, Pallas kernels for 52%

profile of v3, /device:TPU:30, one launch (start us, length us, event | category | flops | bytes accessed | tf_op | source)
XLA Modules:
  0.0 36.8 jit_solution(11188568933805053706)
XLA Ops:
  0.0 1.0 %pack.1.kv_ref.own.after = bf16[544,256]{1,0:T(8,128)(2,1)S(1)} custom-call(bf16[256,1024]{1,0:T(8,128)(2,1)} %q_hbm.3, bf16[256,256]{1,0:T(8,128)(2,1)} %k_hbm.1, bf16[256,256]{1,0:T(8,128)(2,1)} %v_hbm.1), custom_call_target="tpu_custom_call" | custom-call | tf_op jit(solution)/shard_map/pack/pallas_call | solution.py:485
  1.0 1.3 %collective-permute-start = (bf16[544,256]{1,0:T(8,128)(2,1)S(1)}, bf16[544,256]{1,0:T(8,128)(2,1)S(1)}, u32[]{:S(2)}, u32[]{:S(2)}) collective-permute-start(bf16[544,256]{1,0:T(8,128)(2,1)S(1)} %pack.1.kv_ref.own.after), channel_id=1, source_target_pairs={{0,4},{4,8},{8,12},{1,5},{5,9},{9,13},{2,6},{6,10},{10,14},{3,7},{... | collective-permute-start | bytes 835592 | tf_op jit(solution)/shard_map/ppermute | solution.py:461
  2.3 1.8 %taps.1 = (bf16[8,384,256]{2,1,0:T(8,128)(2,1)S(1)}, f32[96,128]{1,0:T(8,128)S(1)}) custom-call(f32[6,8,11]{2,1,0:T(8,128)} %bitcast.3), custom_call_target="tpu_custom_call" | custom-call | flops 1000000000 | bytes 1048576 | tf_op jit(solution)/shard_map/taps/pallas_call | solution.py:511
  4.1 5.8 %own_shard.1 = (bf16[8,256,768]{2,1,0:T(8,128)(2,1)S(1)}, f32[8,256]{1,0:T(8,128)S(1)}, f32[8,256]{1,0:T(8,128)S(1)}, f32[8,128,256]{2,1,0:T(8,128)S(1)}) custom-call(bf16[256,1024]{1,0:T(8,128)(2,1)} %q_hbm.3, bf16[544,256]{1,0:T(8,128)(2,1)S(1)} %pack.1.kv_ref.own.after, bf16[8,384,256]{2,1,0:T(8,128)(2,1)S(1)} %get-tuple-element.24.taps_ref, ...), custom_call_target="tpu_custom_call" | custom-call | flops 6000000000 | bytes 1048576 | tf_op jit(solution)/shard_map/own_shard/pallas_call | solution.py:524
  9.9 1.4 %collective-permute-done.below.body.after = bf16[544,256]{1,0:T(8,128)(2,1)S(1)} collective-permute-done((bf16[544,256]{1,0:T(8,128)(2,1)S(1)}, bf16[544,256]{1,0:T(8,128)(2,1)S(1)}, u32[]{:S(2)}, u32[]{:S(2)}) %collective-permute-start) | collective-permute-done | bytes 278560 | tf_op jit(solution)/shard_map/ppermute | solution.py:461
  11.3 1.3 %collective-permute-start.1 = (bf16[544,256]{1,0:T(8,128)(2,1)S(1)}, bf16[544,256]{1,0:T(8,128)(2,1)S(1)}, u32[]{:S(2)}, u32[]{:S(2)}) collective-permute-start(bf16[544,256]{1,0:T(8,128)(2,1)S(1)} %collective-permute-done.below.body.after), channel_id=1, source_target_pairs={{4,8},{8,12},{5,9},{9,13},{6,10},{10,14},{7,11},{11,15},{20,24},{2... | collective-permute-start | bytes 835592 | tf_op jit(solution)/shard_map/ppermute | solution.py:461
  12.6 0.9 %edge.1 = (bf16[8,256,768]{2,1,0:T(8,128)(2,1)S(1)}, f32[8,32,128]{2,1,0:T(8,128)S(1)}) custom-call(bf16[544,256]{1,0:T(8,128)(2,1)S(1)} %collective-permute-done.below.body.after, bf16[544,256]{1,0:T(8,128)(2,1)S(1)} %pack.1.kv_ref.own.after, f32[96,128]{1,0:T(8,128)S(1)} %get-tuple-element.23.coef, ...), custom_call_target="tpu_custom_call", output_to_operand_aliasing={{0}: (3, {})} | custom-call | flops 1000000000 | bytes 1048576 | tf_op jit(solution)/shard_map/edge/pallas_call | solution.py:554
  13.5 5.2 %shard_step.2 = (f32[8,256]{1,0:T(8,128)S(1)}, f32[8,256]{1,0:T(8,128)S(1)}, f32[8,128,256]{2,1,0:T(8,128)S(1)}) custom-call(bf16[8,256,768]{2,1,0:T(8,128)(2,1)S(1)} %get-tuple-element.26.qcat_ref, bf16[8,384,256]{2,1,0:T(8,128)(2,1)S(1)} %get-tuple-element.24.taps_ref, ...), custom_call_target="tpu_custom_call", output_to_operand_aliasing={{0}: (3, {}), {1}: (4, {}), {2}: (5, {})} | custom-call | flops 5000000000 | bytes 1048576 | tf_op jit(solution)/shard_map/shard_step/pallas_call | solution.py:574
  18.8 2.1 %collective-permute-done.1.body.after = bf16[544,256]{1,0:T(8,128)(2,1)S(1)} collective-permute-done((bf16[544,256]{1,0:T(8,128)(2,1)S(1)}, bf16[544,256]{1,0:T(8,128)(2,1)S(1)}, u32[]{:S(2)}, u32[]{:S(2)}) %collective-permute-start.1) | collective-permute-done | bytes 278560 | tf_op jit(solution)/shard_map/ppermute | solution.py:461
  20.9 1.3 %collective-permute-start.2 = (bf16[544,256]{1,0:T(8,128)(2,1)S(1)}, bf16[544,256]{1,0:T(8,128)(2,1)S(1)}, u32[]{:S(2)}, u32[]{:S(2)}) collective-permute-start(bf16[544,256]{1,0:T(8,128)(2,1)S(1)} %collective-permute-done.1.body.after), channel_id=1, source_target_pairs={{8,12},{9,13},{10,14},{11,15},{24,28},{25,29},{26,30},{27,31}} | collective-permute-start | bytes 835592 | tf_op jit(solution)/shard_map/ppermute | solution.py:461
  22.2 0.0 copy-start
  22.2 0.0 copy-start.1
  22.2 0.0 copy-start.2
  22.2 5.3 %shard_step.3 = (f32[8,256]{1,0:T(8,128)S(1)}, f32[8,256]{1,0:T(8,128)S(1)}, f32[8,128,256]{2,1,0:T(8,128)S(1)}) custom-call(bf16[8,256,768]{2,1,0:T(8,128)(2,1)S(1)} %get-tuple-element.26.qcat_ref, bf16[8,384,256]{2,1,0:T(8,128)(2,1)S(1)} %get-tuple-element.24.taps_ref, ...), custom_call_target="tpu_custom_call", output_to_operand_aliasing={{0}: (3, {}), {1}: (4, {}), {2}: (5, {})} | custom-call | flops 5000000000 | bytes 1048576 | tf_op jit(solution)/shard_map/shard_step/pallas_call | solution.py:574
  27.5 2.1 %collective-permute-done.2.body = bf16[544,256]{1,0:T(8,128)(2,1)S(1)} collective-permute-done((bf16[544,256]{1,0:T(8,128)(2,1)S(1)}, bf16[544,256]{1,0:T(8,128)(2,1)S(1)}, u32[]{:S(2)}, u32[]{:S(2)}) %collective-permute-start.2) | collective-permute-done | bytes 278560 | tf_op jit(solution)/shard_map/ppermute | solution.py:461
  29.6 0.0 copy-done
  29.6 0.0 copy-done.1
  29.6 0.0 copy-done.2
  29.6 7.0 %last_step.1 = bf16[256,1024]{1,0:T(8,128)(2,1)} custom-call(bf16[8,256,768]{2,1,0:T(8,128)(2,1)S(1)} %get-tuple-element.26.qcat_ref, bf16[8,384,256]{2,1,0:T(8,128)(2,1)S(1)} %get-tuple-element.24.taps_ref, f32[8,32,128]{2,1,0:T(8,128)S(1)} %get-tuple-element.27.corner_ref, f32[8,256]{1,0:T(8,128)S(1)} %get-tuple-element.37.m_in, ...), custom_call_target="tpu_custom_call" | custom-call | flops 5000000000 | bytes 1048576 | tf_op jit(solution)/shard_map/last_step/pallas_call | solution.py:586
Async XLA Ops:
  1.0 10.3 %collective-permute-start = (bf16[544,256]{1,0:T(8,128)(2,1)S(1)}, bf16[544,256]{1,0:T(8,128)(2,1)S(1)}, u32[]{:S(2)}, u32[]{:S(2)}) collective-permute-start(bf16[544,256]{1,0:T(8,128)(2,1)S(1)} %pack.1.kv_ref.own.after), channel_id=1, source_target_pairs={{0,4},{4,8},{8,12},{1,5},{5,9},{9,13},{2,6},{6,10},{10,14},{3,7},{... | collective-permute-start | bytes 835592 | tf_op jit(solution)/shard_map/ppermute | solution.py:461
  11.3 9.5 %collective-permute-start.1 = (bf16[544,256]{1,0:T(8,128)(2,1)S(1)}, bf16[544,256]{1,0:T(8,128)(2,1)S(1)}, u32[]{:S(2)}, u32[]{:S(2)}) collective-permute-start(bf16[544,256]{1,0:T(8,128)(2,1)S(1)} %collective-permute-done.below.body.after), channel_id=1, source_target_pairs={{4,8},{8,12},{5,9},{9,13},{6,10},{10,14},{7,11},{11,15},{20,24},{2... | collective-permute-start | bytes 835592 | tf_op jit(solution)/shard_map/ppermute | solution.py:461
  20.9 8.7 %collective-permute-start.2 = (bf16[544,256]{1,0:T(8,128)(2,1)S(1)}, bf16[544,256]{1,0:T(8,128)(2,1)S(1)}, u32[]{:S(2)}, u32[]{:S(2)}) collective-permute-start(bf16[544,256]{1,0:T(8,128)(2,1)S(1)} %collective-permute-done.1.body.after), channel_id=1, source_target_pairs={{8,12},{9,13},{10,14},{11,15},{24,28},{25,29},{26,30},{27,31}} | collective-permute-start | bytes 835592 | tf_op jit(solution)/shard_map/ppermute | solution.py:461
  22.2 7.4 %copy-start = (f32[1024]{0:T(1024)S(1)}, f32[1024]{0:T(1024)}, u32[]{:S(2)}) copy-start(f32[1024]{0:T(1024)} %param.12) | copy-start | bytes 12292
  22.2 7.4 %copy-start.1 = (f32[2,4,4]{2,1,0:T(4,128)S(1)}, f32[2,4,4]{2,1,0:T(4,128)}, u32[]{:S(2)}) copy-start(f32[2,4,4]{2,1,0:T(4,128)} %mix_ref.1) | copy-start | bytes 388
  22.2 7.4 %copy-start.2 = (s32[2]{0:T(128)S(1)}, s32[2]{0:T(128)}, u32[]{:S(2)}) copy-start(s32[2]{0:T(128)} %bounds_ref.1) | copy-start | bytes 28
